TPU v7x, 32 devices: a whole 2x2x4 slice. The times are simulated.
32 devices in a mesh: band: 16 (over z, y, x), lev: 2 (over core).
Axes of the slice: x: 2, y: 2, z: 4, core: 2. Of those that a mesh axis runs over, the one named last changes fastest.
Arguments:
- arrival_adjoint: bfloat16 [160, 64, 1536], P('band', 'lev'), may hold values from -6 to 6
- interp_tiles: bfloat16 [160, 12, 128, 128], P('band'), may hold values from -0.5 to 0.5
- departure_block: int32 [160, 12], P('band'), may hold values from 0 to 239
- slot_wavenumber: int32 [768], replicated, may hold values from 0 to 767, each once
- legendre: bfloat16 [768, 160, 768], P('band', None, 'lev'), may hold values from -0.5 to 0.5
Outputs:
- spectral: bfloat16 [768, 64, 2, 768], P('band', None, None, 'lev')
Inputs may be any that keep to these rules, and one draw needn't show every extreme that they name: `departure_block`: an entry d of the tile at latitude l names latitude L + d // 12 - 5 and longitude block d % 12, where L is the first latitude of l's band of 10. `slot_wavenumber`: each wavenumber below 768 stands in exactly one slot.
All inputs are finite; a program needn't handle non-finite values.
Results may differ from a plain program's by a relative error of at most 0.015.
Values may be sent and summed in bfloat16 or wider, within the bound.
No kernel may reach another device: no remote copies, remote signals or barrier semaphores. Data moves between devices by JAX's collectives and lax.ppermute only.
A program may use at most 128 MiB of HBM per device.

v0:
```python
import math

import jax
import jax.numpy as jnp
from jax import lax
from jax.sharding import PartitionSpec as P


def passed_along(block, axis, distance):
    devices = range(lax.axis_size(axis))
    route = [(i - distance, i) for i in devices if i - distance in devices]
    return lax.ppermute(block, axis, route)


def wave_table(slot_wavenumber, lon_count):
    column = lax.iota(jnp.int32, lon_count)[:, None]
    product = column * slot_wavenumber[None, :] % lon_count
    angle = product.astype(jnp.float32) * (2.0 * math.pi / lon_count)
    factor = math.sqrt(2.0 / lon_count)
    return jnp.stack([jnp.cos(angle) * factor, jnp.sin(angle) * factor]).astype(jnp.bfloat16)


def local(arrival_adjoint, interp_tiles, departure_block, slot_wavenumber, legendre):
    lat_count, level_count, lon_count = arrival_adjoint.shape
    block_count = interp_tiles.shape[1]
    tile_width = interp_tiles.shape[2]
    rim_rows = lat_count // 2
    tiles = arrival_adjoint.reshape(lat_count, level_count, block_count, tile_width)
    contrib = jnp.einsum("lvbi,lbik->lbvk", tiles, interp_tiles, preferred_element_type=jnp.float32)
    contrib = contrib.reshape(lat_count * block_count, level_count * tile_width)
    upper = contrib.astype(jnp.bfloat16)
    lower = (contrib - upper.astype(jnp.float32)).astype(jnp.bfloat16)
    extended = (lat_count + 2 * rim_rows) * block_count
    targets = (lax.iota(jnp.int32, extended)[:, None] == departure_block.reshape(1, -1)).astype(
        jnp.bfloat16
    )
    placed = jnp.dot(targets, upper, preferred_element_type=jnp.float32) + jnp.dot(
        targets, lower, preferred_element_type=jnp.float32
    )
    placed = placed.reshape(lat_count + 2 * rim_rows, block_count, level_count, tile_width)
    from_below = passed_along(
        placed[lat_count + rim_rows :].astype(jnp.bfloat16), "band", 1
    ).astype(jnp.float32)
    from_above = passed_along(placed[:rim_rows].astype(jnp.bfloat16), "band", -1).astype(
        jnp.float32
    )
    grid = placed[rim_rows : rim_rows + lat_count] + jnp.concatenate(
        [from_below, from_above], axis=0
    )
    grid = grid.astype(jnp.bfloat16)
    table = wave_table(slot_wavenumber, lon_count).reshape(2, block_count, tile_width, -1)
    fourier = jnp.einsum("lbvt,cbts->scvl", grid, table, preferred_element_type=jnp.float32).astype(
        jnp.bfloat16
    )
    wave_count = fourier.shape[0]
    flat = fourier.reshape(wave_count, -1)
    shared = lax.all_gather(flat[None], "lev", axis=0, tiled=True)
    owned = lax.all_to_all(shared, "band", split_axis=1, concat_axis=2, tiled=True)
    group_count = owned.shape[0]
    slot_count = owned.shape[1]
    band_count = lax.axis_size("band")
    degree_count = legendre.shape[2]
    owned = owned.reshape(group_count, slot_count, band_count, 2, level_count, lat_count)
    tables = legendre.reshape(slot_count, band_count, lat_count, degree_count)
    spectral = jnp.einsum("gsbcvl,sbln->sgvcn", owned, tables, preferred_element_type=jnp.float32)
    spectral = spectral.reshape(slot_count, group_count * level_count, 2, degree_count)
    degree = lax.axis_index("lev") * degree_count + lax.iota(jnp.int32, degree_count)
    owned_waves = lax.dynamic_slice_in_dim(
        slot_wavenumber, lax.axis_index("band") * slot_count, slot_count
    )
    keep = degree[None, :] >= owned_waves[:, None]
    return jnp.where(keep[:, None, None, :], spectral, 0.0).astype(jnp.bfloat16)


def solution(mesh):
    placed = (
        P("band", "lev", None),
        P("band", None, None, None),
        P("band", None),
        P(),
        P("band", None, "lev"),
    )
    return jax.shard_map(
        local, mesh=mesh, in_specs=placed, out_specs=P("band", None, None, "lev"), check_vma=False
    )
```

profile of v0, /device:TPU:12, one launch (start us, length us, event | category | flops | bytes accessed | tf_op | source)
XLA Modules:
  0.0 174.6 jit_solution(13239174042174371197)
XLA Ops:
  6.5 0.0 copy-start
  6.5 0.0 all-gather.2.cloned.1.call-start
  6.5 0.9 eq.18
  7.4 0.4 copy-done
  7.8 3.2 %fusion.20 = f32[10,12,32,128]{3,2,1,0:T(8,128)S(1)} fusion(bf16[10,12,128,128]{3,2,1,0:T(8,128)(2,1)} %param.6, bf16[10,32,1536]{2,1,0:T(8,128)(2,1)S(1)} %copy-done), kind=kOutput, calls=%fused_computation.28 | convolution fusion | flops 125829120 | bytes 6881280 | tf_op jit(solution)/shard_map/lvbi,lbik->lbvk/dot_general | solution.py:29
  11.0 1.5 fusion.15
  12.5 1.6 fusion.30
  14.2 0.1 fusion.29
  14.3 0.1 copy.44
  14.4 3.4 %collective-permute-start = (bf16[5,12,32,128]{3,2,1,0:T(8,128)(2,1)S(1)}, bf16[5,12,32,128]{3,2,1,0:T(8,128)(2,1)S(1)}, u32[]{:S(2)}, u32[]{:S(2)}) collective-permute-start(bf16[5,12,32,128]{3,2,1,0:T(8,128)(2,1)S(1)} %bitcast.81), channel_id=1, source_target_pairs={{0,2},{2,4},{4,6},{6,8},{8,10},{10,12},{12,14},{14,16},{16,18},{18... | collective-permute-start | bytes 1474568 | tf_op jit(solution)/shard_map/ppermute | solution.py:12
  17.8 0.1 copy.45
  18.0 3.3 %collective-permute-start.1 = (bf16[5,12,32,128]{3,2,1,0:T(8,128)(2,1)S(1)}, bf16[5,12,32,128]{3,2,1,0:T(8,128)(2,1)S(1)}, u32[]{:S(2)}, u32[]{:S(2)}) collective-permute-start(bf16[5,12,32,128]{3,2,1,0:T(8,128)(2,1)S(1)} %bitcast.82), channel_id=1, source_target_pairs={{2,0},{4,2},{6,4},{8,6},{10,8},{12,10},{14,12},{16,14},{18,16},{20... | collective-permute-start | bytes 1474568 | tf_op jit(solution)/shard_map/ppermute | solution.py:12
  21.3 0.0 copy-start.2
  21.4 0.1 slice_bitcast_fusion
  21.5 0.3 copy.43
  21.9 0.2 copy-done.2
  22.0 20.6 %multiply_convert_fusion.1 = (bf16[1,12,128,768]{3,2,1,0:T(8,128)(2,1)S(1)}, bf16[1,12,128,768]{3,2,1,0:T(8,128)(2,1)S(1)}) fusion(s32[768]{0:T(1024)S(1)} %copy-done.2, s32[12,128]{1,0:T(8,128)S(1)} %multiply_add_fusion), kind=kLoop, calls=%fused_computation.13 | loop fusion | flops 15335424 | bytes 4727808 | tf_op jit(solution)/shard_map/convert.3
  42.6 0.0 collective-permute-done
  42.6 0.0 collective-permute-done.1
  42.6 1.7 fusion.16
  44.3 0.6 copy.25
  44.9 0.4 broadcast_in_dim_reshape.3
  45.3 1.3 copy.26
  46.6 0.0 all-gather.2.cloned.1.call-update
  46.7 11.0 %all-gather.2.cloned.1.call-done = bf16[2,768,640]{2,1,0:T(8,128)(2,1)} async-done(((bf16[1,768,640]{2,1,0:T(8,128)(2,1)}), bf16[2,768,640]{2,1,0:T(8,128)(2,1)}) %all-gather.2.cloned.1.call-update) | async-done | bytes 1966096 | tf_op jit(solution)/shard_map/all_gather | solution.py:57
  57.7 4.8 %copy.27 = bf16[2,768,640]{2,0,1:T(2,128)(2,1)} copy(bf16[2,768,640]{2,1,0:T(8,128)(2,1)} %all-gather.2.cloned.1.call-done) | data formatting | bytes 3932160 | tf_op jit(solution)/shard_map/all_gather | solution.py:57
  62.6 7.0 %all-to-all-start = ((bf16[2,768,640]{2,0,1:T(2,128)(2,1)}), bf16[2,768,640]{2,0,1:T(2,128)(2,1)S(1)}, u32[]{:S(2)}, u32[]{:S(2)}) async-start(bf16[2,768,640]{2,0,1:T(2,128)(2,1)} %copy.27), calls=%async_computation | async-start | bytes 3932160 | tf_op jit(solution)/shard_map/all_to_all | solution.py:58
  69.5 7.4 %copy.30 = bf16[48,160,384]{2,0,1:T(8,128)(2,1)} copy(bf16[48,160,384]{2,1,0:T(8,128)(2,1)} %param.9) | data formatting | bytes 11796480 | tf_op args[4]
  77.0 0.1 dynamic_slice.3
  77.0 0.1 broadcast_compare_fusion
  77.1 38.1 %all-to-all-done = bf16[2,768,640]{2,0,1:T(2,128)(2,1)S(1)} async-done(((bf16[2,768,640]{2,0,1:T(2,128)(2,1)}), bf16[2,768,640]{2,0,1:T(2,128)(2,1)S(1)}, u32[]{:S(2)}, u32[]{:S(2)}) %all-to-all-start) | async-done | bytes 1966112 | tf_op jit(solution)/shard_map/all_to_all | solution.py:58
  115.3 1.5 copy.28
  116.8 6.7 %copy.29 = bf16[2,48,16,640]{1,2,3,0:T(8,128)(2,1)} copy(bf16[2,48,16,640]{3,1,2,0:T(8,128)(2,1)} %bitcast.75) | data formatting | bytes 3932160 | tf_op jit(solution)/shard_map/all_to_all | solution.py:58
  123.5 15.3 %copy.31 = bf16[2,48,16,2,32,10]{4,2,5,3,0,1:T(8,128)(2,1)} copy(bf16[2,48,16,2,32,10]{1,2,5,4,3,0:T(8,128)(2,1)} %bitcast.72) | data formatting | bytes 3932160 | tf_op jit(solution)/shard_map/reshape | solution.py:63
  138.9 12.0 %fusion.11 = bf16[48,2,32,2,384]{4,2,3,1,0:T(8,128)(2,1)} fusion(bf16[2,48,16,2,32,10]{4,2,5,3,0,1:T(8,128)(2,1)} %copy.31, bf16[48,16,10,384,1,1]{3,0,2,1,5,4:T(8,128)(2,1)} %bitcast.71), kind=kOutput, calls=%fused_computation.18 | convolution fusion | flops 754974720 | bytes 12582912 | tf_op jit(solution)/shard_map/gsbcvl,sbln->sgvcn/dot_general | solution.py:65
  150.9 3.2 %copy.33 = bf16[48,2,32,2,384]{4,2,1,3,0:T(8,128)(2,1)S(1)} copy(bf16[48,2,32,2,384]{4,2,3,1,0:T(8,128)(2,1)} %fusion.11) | data formatting | bytes 9437184 | tf_op jit(solution)/shard_map/gsbcvl,sbln->sgvcn/transpose | solution.py:65
  154.1 0.0 copy-start.1
  154.1 4.2 %fusion = bf16[48,64,2,384]{3,1,2,0:T(8,128)(2,1)} fusion(bf16[48,2,32,2,384]{4,2,1,3,0:T(8,128)(2,1)S(1)} %copy.33, pred[48,384]{1,0:T(8,128)(4,1)S(1)} %broadcast_compare_fusion), kind=kLoop, calls=%fused_computation.1 | loop fusion | flops 2359296 | bytes 9455616 | tf_op jit(solution)/shard_map/convert_element_type | solution.py:72
  158.4 9.4 %copy.34 = bf16[48,64,2,384]{3,2,1,0:T(2,128)(2,1)} copy(bf16[48,64,2,384]{3,1,2,0:T(8,128)(2,1)} %fusion) | data formatting | bytes 9437184 | tf_op jit(solution)/shard_map/convert_element_type | solution.py:72
  167.7 0.0 copy-done.1
  (4 shorter events, 0.1 us)
Async XLA Ops:
  6.5 1.2 copy-start
  6.5 51.2 %all-gather.2.cloned.1.call-start = ((), (), s32[]{:S(2)}) async-start(), calls=%async_computation.1 | async-start | bytes 2949120 | tf_op jit(solution)/shard_map/all_gather | solution.py:57
  14.4 28.2 %collective-permute-start = (bf16[5,12,32,128]{3,2,1,0:T(8,128)(2,1)S(1)}, bf16[5,12,32,128]{3,2,1,0:T(8,128)(2,1)S(1)}, u32[]{:S(2)}, u32[]{:S(2)}) collective-permute-start(bf16[5,12,32,128]{3,2,1,0:T(8,128)(2,1)S(1)} %bitcast.81), channel_id=1, source_target_pairs={{0,2},{2,4},{4,6},{6,8},{8,10},{10,12},{12,14},{14,16},{16,18},{18... | collective-permute-start | bytes 1474568 | tf_op jit(solution)/shard_map/ppermute | solution.py:12
  18.0 24.7 %collective-permute-start.1 = (bf16[5,12,32,128]{3,2,1,0:T(8,128)(2,1)S(1)}, bf16[5,12,32,128]{3,2,1,0:T(8,128)(2,1)S(1)}, u32[]{:S(2)}, u32[]{:S(2)}) collective-permute-start(bf16[5,12,32,128]{3,2,1,0:T(8,128)(2,1)S(1)} %bitcast.82), channel_id=1, source_target_pairs={{2,0},{4,2},{6,4},{8,6},{10,8},{12,10},{14,12},{16,14},{18,16},{20... | collective-permute-start | bytes 1474568 | tf_op jit(solution)/shard_map/ppermute | solution.py:12
  21.3 0.7 copy-start.2
  62.6 52.7 %all-to-all-start = ((bf16[2,768,640]{2,0,1:T(2,128)(2,1)}), bf16[2,768,640]{2,0,1:T(2,128)(2,1)S(1)}, u32[]{:S(2)}, u32[]{:S(2)}) async-start(bf16[2,768,640]{2,0,1:T(2,128)(2,1)} %copy.27), calls=%async_computation | async-start | bytes 3932160 | tf_op jit(solution)/shard_map/all_to_all | solution.py:58
  154.1 13.6 %copy-start.1 = (bf16[10,32,1536]{2,1,0:T(8,128)(2,1)S(1)}, bf16[10,32,1536]{2,1,0:T(8,128)(2,1)}, u32[]{:S(2)}) copy-start(bf16[10,32,1536]{2,1,0:T(8,128)(2,1)} %param.5) | copy-start | bytes 2949124
Sparse Core Ops, SparseCore 0:
  46.8 10.8 all-gather.1
where the time goes:
time: 175 us
  local copies, waits for them, and re-layouts  53.1 us (30%)
  waiting for transfers between devices  49.2 us (28%)
  other arithmetic  24.9 us (14%)
  matrix products  20.1 us (11%)
  starting transfers between devices  13.7 us (8%)
  between operations  13.6 us (8%)
    all_to_all x1, waiting for transfers between devices, local(): lax.all_to_all(shared, 'band', split_axis=1, concat_axis=2, tiled=True)  38.1 us
    another operation x1, other arithmetic  20.6 us
    reshape x1, local copies, waits for them, and re-layouts, local(): owned.reshape(group_count, slot_count, band_count, 2, level_count, lat_co...  15.3 us
    dot_general x1, matrix products, local(): jnp.einsum('gsbcvl,sbln->sgvcn', owned, tables, preferred_element_type=jn...  12 us
    all_gather x1, waiting for transfers between devices, local(): shared = lax.all_gather(flat[None], 'lev', axis=0, tiled=True)  11 us
    convert_element_type x1, local copies, waits for them, and re-layouts, local(): return jnp.where(keep[:, None, None, :], spectral, 0.0).astype(jnp.bfloat16)  9.37 us
    unnamed x13, local copies, waits for them, and re-layouts  8.71 us
    all_to_all x2, local copies, waits for them, and re-layouts, local(): lax.all_to_all(shared, 'band', split_axis=1, concat_axis=2, tiled=True)  8.26 us
  transfers between devices with their start and end apart: 4, of which 2 were waited for; matrix products, arithmetic and copies ran while one was open for 16% of the time, Pallas kernels for 0%

commit v1 on v0

v1 whole, which is shorter than its diff:
```python
import functools
import math

import jax
import jax.numpy as jnp
from jax import lax
from jax.experimental import pallas as pl
from jax.experimental.pallas import tpu as pltpu
from jax.sharding import PartitionSpec as P

BF = jnp.bfloat16
F32 = jnp.float32
LANES = 128
VMEM_LIMIT = 48 * 2**20


def passed_along(block, axis, distance):
    devices = range(lax.axis_size(axis))
    route = [(i - distance, i) for i in devices if i - distance in devices]
    return lax.ppermute(block, axis, route)


def whole(shape):
    return pl.BlockSpec(shape, lambda *_: (0,) * len(shape))


def interpolate_kernel(rim, depart, arrival, tiles, below, mid, above, sums):
    lat = pl.program_id(0)
    blocks, width = tiles.shape[1], tiles.shape[2]

    @pl.when(lat == 0)
    def _():
        sums[...] = jnp.zeros_like(sums)

    contrib = [
        jnp.dot(
            arrival[0, :, b * width : (b + 1) * width], tiles[0, b], preferred_element_type=F32
        )
        for b in range(blocks)
    ]
    for b in range(blocks):
        target = depart[lat * blocks + b]
        sums[target] += contrib[b]

    @pl.when(lat == pl.num_programs(0) - 1)
    def _():
        below[...] = sums[:rim].astype(BF)
        above[...] = sums[sums.shape[0] - rim :].astype(BF)
        mid[...] = sums[rim : sums.shape[0] - rim]


def interpolate(arrival, tiles, depart):
    lats, levels, lons = arrival.shape
    blocks, width = tiles.shape[1], tiles.shape[2]
    rim = lats // 2 * blocks
    segments = lats * blocks + 2 * rim
    grid_spec = pltpu.PrefetchScalarGridSpec(
        num_scalar_prefetch=1,
        grid=(lats,),
        in_specs=[
            pl.BlockSpec((1, levels, lons), lambda i, d: (i, 0, 0)),
            pl.BlockSpec((1, blocks, width, width), lambda i, d: (i, 0, 0, 0)),
        ],
        out_specs=[
            whole((rim, levels, width)),
            whole((segments - 2 * rim, levels, width)),
            whole((rim, levels, width)),
        ],
        scratch_shapes=[pltpu.VMEM((segments, levels, width), F32)],
    )
    return pl.pallas_call(
        functools.partial(interpolate_kernel, rim),
        grid_spec=grid_spec,
        out_shape=[
            jax.ShapeDtypeStruct((rim, levels, width), BF),
            jax.ShapeDtypeStruct((segments - 2 * rim, levels, width), F32),
            jax.ShapeDtypeStruct((rim, levels, width), BF),
        ],
        compiler_params=pltpu.CompilerParams(vmem_limit_bytes=VMEM_LIMIT),
        cost_estimate=pl.CostEstimate(
            flops=2 * lats * levels * lons * width,
            bytes_accessed=2 * (arrival.size + tiles.size),
            transcendentals=0,
        ),
        name="interpolate",
    )(depart.reshape(-1), arrival, tiles)


def table_kernel(lons, waves, table):
    blocks = lons // LANES
    rows = waves.shape[1]
    wave = waves[0].astype(F32)
    lane = lax.broadcasted_iota(jnp.int32, (rows, LANES), 1).astype(F32)
    product = lane * wave

    def turn(steps, period):
        left = steps - period * jnp.floor((steps + 0.5) * (1.0 / period))
        angle = left * (2.0 * math.pi / period)
        return jnp.cos(angle), jnp.sin(angle)

    fine_cos, fine_sin = turn(product, float(lons))
    coarse_cos, coarse_sin = turn(product, float(blocks))
    factor = math.sqrt(2.0 / lons)
    coarse_cos = coarse_cos * factor
    coarse_sin = coarse_sin * factor
    for b in range(blocks):
        cos_b, sin_b = coarse_cos[:, b : b + 1], coarse_sin[:, b : b + 1]
        at = slice(b * LANES, (b + 1) * LANES)
        table[0, 0, :, at] = (cos_b * fine_cos - sin_b * fine_sin).astype(BF)
        table[0, 1, :, at] = (sin_b * fine_cos + cos_b * fine_sin).astype(BF)


def wave_table(waves, lons):
    halves, count, _ = waves.shape
    rows = 128
    return pl.pallas_call(
        functools.partial(table_kernel, lons),
        grid=(halves, count // rows),
        in_specs=[pl.BlockSpec((1, rows, 1), lambda h, i: (h, i, 0))],
        out_specs=pl.BlockSpec((1, 2, rows, lons), lambda h, i: (h, 0, i, 0)),
        out_shape=jax.ShapeDtypeStruct((halves, 2, count, lons), BF),
        compiler_params=pltpu.CompilerParams(vmem_limit_bytes=VMEM_LIMIT),
        cost_estimate=pl.CostEstimate(
            flops=40 * halves * count * lons, bytes_accessed=4 * halves * count * lons, transcendentals=0
        ),
        name="table",
    )(waves)


def fourier_kernel(mid, from_below, from_above, table, sent, grid, sums):
    segments, levels, width = mid.shape
    rim = from_below.shape[0]
    lats, _ = sent.shape[1], sent.shape[3]
    blocks = segments // lats
    per_row = LANES // levels
    parts = table.shape[0]
    groups = pl.cdiv(lats, per_row)
    half = sent.shape[2]

    @pl.when(pl.program_id(0) == 0)
    def _():
        for lat in range(groups * per_row):
            group, place = lat // per_row, lat % per_row
            for b in range(blocks):
                seg = lat * blocks + b
                if lat >= lats:
                    row = jnp.zeros((levels, width), BF)
                else:
                    add = from_below[seg] if seg < rim else from_above[seg - rim]
                    row = (mid[seg] + add.astype(F32)).astype(BF)
                for k in range(parts):
                    start = group * LANES + (place + k) % per_row * levels
                    grid[k, start : start + levels, b * width : (b + 1) * width] = row

    for k in range(parts):
        sums[k] = lax.dot_general(
            table[k], grid[k], (((1,), (1,)), ((), ())), preferred_element_type=F32
        )
    lane = lax.broadcasted_iota(jnp.int32, (half, LANES), 1) // levels
    for d in range(sent.shape[0]):
        for group in range(groups):
            held = [
                sums[k, d * half : (d + 1) * half, group * LANES : (group + 1) * LANES]
                for k in range(parts)
            ]
            for place in range(per_row):
                lat = group * per_row + place
                if lat >= lats:
                    continue
                row = held[(0 - place) % per_row]
                for p in range(1, per_row):
                    row = jnp.where(lane == p, held[(p - place) % per_row], row)
                if place:
                    row = pltpu.roll(row, LANES - place * levels, 1)
                sent[d, lat] = row.astype(BF)


def fourier(mid, from_below, from_above, table, bands):
    segments, levels, width = mid.shape
    halves, _, count, lons = table.shape
    lats = segments * width // lons
    half = count // bands
    parts = 2 * halves
    steps = 2
    rows = count // steps
    groups = pl.cdiv(lats * levels, LANES)
    return pl.pallas_call(
        fourier_kernel,
        grid=(steps,),
        in_specs=[
            whole(mid.shape),
            whole(from_below.shape),
            whole(from_above.shape),
            pl.BlockSpec((parts, rows, lons), lambda i: (0, i, 0)),
        ],
        out_specs=pl.BlockSpec((bands // steps, lats, half, LANES), lambda i: (i, 0, 0, 0)),
        out_shape=jax.ShapeDtypeStruct((bands, lats, half, LANES), BF),
        scratch_shapes=[
            pltpu.VMEM((parts, groups * LANES, lons), BF),
            pltpu.VMEM((parts, rows, groups * LANES), F32),
        ],
        compiler_params=pltpu.CompilerParams(vmem_limit_bytes=VMEM_LIMIT),
        cost_estimate=pl.CostEstimate(
            flops=4 * halves * count * lons * lats * levels,
            bytes_accessed=4 * halves * count * lons,
            transcendentals=0,
        ),
        name="fourier",
    )(mid, from_below, from_above, table.reshape(parts, count, lons))


def legendre_kernel(per_step, waves, place, own, other, leg_a, leg_b, out, first, second):
    step = pl.program_id(0)
    lats, half, lanes = own.shape
    levels = lanes // 4
    degrees = leg_a.shape[2]
    lev = place[0]

    @pl.when(step == 0)
    def _():
        @pl.when(lev == 0)
        def _():
            first[...] = own[...].astype(F32).reshape(first.shape)
            second[...] = other[...].astype(F32).reshape(first.shape)

        @pl.when(lev != 0)
        def _():
            first[...] = other[...].astype(F32).reshape(first.shape)
            second[...] = own[...].astype(F32).reshape(first.shape)

    lane = lax.broadcasted_iota(jnp.int32, (lats, lanes), 1)
    column = lax.broadcasted_iota(jnp.int32, (levels, degrees), 1) + lev * degrees
    for i in range(per_step):
        r = step * per_step + i
        x0 = first[pl.ds(r, lats, stride=half), :]
        x1 = second[pl.ds(r, lats, stride=half), :]
        for slot in range(2):
            low, high = (x0, x1) if slot == 0 else (x1, x0)
            joined = jnp.where(lane < lanes // 2, low, high).astype(BF)
            leg = (leg_a, leg_b)[slot][i]
            sums = lax.dot_general(
                joined, leg, (((0,), (0,)), ((), ())), preferred_element_type=F32
            )
            keep = column >= waves[slot * half + r]
            for side in range(2):
                for part in range(2):
                    at = (side * 2 + part) * levels
                    level = (side ^ slot) * levels
                    out[slot, i, level : level + levels, part, :] = jnp.where(
                        keep, sums[at : at + levels], 0.0
                    ).astype(BF)


def legendre_sums(own, other, legendre, waves, lev):
    slots, lats, degrees = legendre.shape
    half, lanes = slots // 2, own.shape[3]
    per_step = math.gcd(half, 4)
    shape = (lats, half, lanes)
    grid_spec = pltpu.PrefetchScalarGridSpec(
        num_scalar_prefetch=2,
        grid=(half // per_step,),
        in_specs=[
            whole(shape),
            whole(shape),
            pl.BlockSpec((per_step, lats, degrees), lambda i, *_: (i, 0, 0)),
            pl.BlockSpec((per_step, lats, degrees), lambda i, *_: (i + half // per_step, 0, 0)),
        ],
        out_specs=pl.BlockSpec(
            (2, per_step, lanes // 2, 2, degrees), lambda i, *_: (0, i, 0, 0, 0)
        ),
        scratch_shapes=[
            pltpu.VMEM((lats * half, lanes), F32),
            pltpu.VMEM((lats * half, lanes), F32),
        ],
    )
    out = pl.pallas_call(
        functools.partial(legendre_kernel, per_step),
        grid_spec=grid_spec,
        out_shape=jax.ShapeDtypeStruct((2, half, lanes // 2, 2, degrees), BF),
        compiler_params=pltpu.CompilerParams(vmem_limit_bytes=VMEM_LIMIT),
        cost_estimate=pl.CostEstimate(
            flops=2 * slots * lats * lanes * degrees,
            bytes_accessed=2 * legendre.size + 2 * slots * lanes * degrees,
            transcendentals=0,
        ),
        name="legendre_sums",
    )(waves, lev, own.reshape(shape), other.reshape(shape), legendre, legendre)
    return out.reshape(slots, lanes // 2, 2, degrees)


def local(arrival_adjoint, interp_tiles, departure_block, slot_wavenumber, legendre):
    lons = arrival_adjoint.shape[2]
    slots = legendre.shape[0]
    bands = lax.axis_size("band")
    lev = lax.axis_index("lev")
    to_below, mid, to_above = interpolate(arrival_adjoint, interp_tiles, departure_block)
    from_below = passed_along(to_above, "band", 1)
    from_above = passed_along(to_below, "band", -1)
    pairs = slot_wavenumber.reshape(bands, 2, slots // 2).transpose(1, 0, 2)
    pairs = jnp.where(lev == 0, pairs, pairs[::-1])
    table = wave_table(pairs.reshape(2, -1, 1), lons)
    sent = fourier(mid, from_below, from_above, table, bands)
    own = lax.all_to_all(sent, "band", split_axis=0, concat_axis=0)
    other = lax.ppermute(own, "lev", [(0, 1), (1, 0)])
    waves = lax.dynamic_slice_in_dim(slot_wavenumber, lax.axis_index("band") * slots, slots)
    return legendre_sums(own, other, legendre, waves, lev.reshape(1))


def solution(mesh):
    placed = (
        P("band", "lev", None),
        P("band", None, None, None),
        P("band", None),
        P(),
        P("band", None, "lev"),
    )
    return jax.shard_map(
        local, mesh=mesh, in_specs=placed, out_specs=P("band", None, None, "lev"), check_vma=False
    )
```

time: 175 us -> 88 us (0.50)
  the two profiles are of different devices: /device:TPU:12 before, /device:TPU:1 now
where the time goes in v1:
time: 88 us; the launch traced here: 87.1 us
  Pallas kernels  30.4 us (35%)
  blocking collectives  29.8 us (34%)
  waiting for transfers between devices  14.4 us (16%)
  starting transfers between devices  7.91 us (9%)
  local copies, waits for them, and re-layouts  4.55 us (5%)
    all_to_all x1, blocking collectives, local(): own = lax.all_to_all(sent, 'band', split_axis=0, concat_axis=0)  29.8 us
    ppermute x2, waiting for transfers between devices, passed_along(): return lax.ppermute(block, axis, route)  12.2 us
    pallas_call x1, Pallas kernels, legendre_sums(): pl.pallas_call(functools.partial(legendre_kernel, per_step), grid_spec=gr...  9.63 us
    pallas_call x1, Pallas kernels, interpolate(): pl.pallas_call(functools.partial(interpolate_kernel, rim), grid_spec=grid...  8.44 us
    pallas_call x1, Pallas kernels, wave_table(): pl.pallas_call(functools.partial(table_kernel, lons), grid=(halves, count...  6.44 us
    pallas_call x1, Pallas kernels, fourier(): pl.pallas_call(fourier_kernel, grid=(steps,), in_specs=[whole(mid.shape),...  5.89 us
    ppermute x2, starting transfers between devices, passed_along(): return lax.ppermute(block, axis, route)  5.25 us
    unnamed x6, local copies, waits for them, and re-layouts  3.39 us
  transfers between devices with their start and end apart: 3, of which 3 were waited for; matrix products, arithmetic and copies ran while one was open for 0% of the time, Pallas kernels for 7%

profile of v1, /device:TPU:1, one launch (start us, length us, event | category | flops | bytes accessed | tf_op | source)
XLA Modules:
  0.0 87.1 jit_solution(17933632639081334615)
XLA Ops:
  0.0 0.0 copy-start.2
  0.0 0.8 reshape.25.depart
  0.8 0.0 copy-start.1
  0.8 1.2 %copy-done.1 = bf16[10,32,1536]{2,1,0:T(8,128)(2,1)S(1)} copy-done((bf16[10,32,1536]{2,1,0:T(8,128)(2,1)S(1)}, bf16[10,32,1536]{2,1,0:T(8,128)(2,1)}, u32[]{:S(2)}) %copy-start.1) | copy-done | bytes 983064
  2.0 8.4 %interpolate.1 = (bf16[60,32,128]{2,1,0:T(8,128)(2,1)}, f32[120,32,128]{2,1,0:T(8,128)S(1)}, bf16[60,32,128]{2,1,0:T(8,128)(2,1)}) custom-call(s32[120]{0:T(128)S(1)} %reshape.25.depart, bf16[10,32,1536]{2,1,0:T(8,128)(2,1)S(1)} %copy-done.1, bf16[10,12,128,128]{3,2,1,0:T(8,128)(2,1)} %tiles.1), custom_call_target="tpu_custom_call" | custom-call | flops 125829120 | bytes 4915200 | tf_op jit(solution)/shard_map/interpolate/pallas_call | solution.py:71
  10.4 4.0 %collective-permute-start = (bf16[60,32,128]{2,1,0:T(8,128)(2,1)}, bf16[60,32,128]{2,1,0:T(8,128)(2,1)S(1)}, u32[]{:S(2)}, u32[]{:S(2)}) collective-permute-start(bf16[60,32,128]{2,1,0:T(8,128)(2,1)} %get-tuple-element.9), channel_id=1, source_target_pairs={{0,2},{2,4},{4,6},{6,8},{8,10},{10,12},{12,14},{14,16},{16,18},{18... | collective-permute-start | bytes 1474568 | tf_op jit(solution)/shard_map/ppermute | solution.py:20
  14.4 1.3 %collective-permute-start.1 = (bf16[60,32,128]{2,1,0:T(8,128)(2,1)}, bf16[60,32,128]{2,1,0:T(8,128)(2,1)S(1)}, u32[]{:S(2)}, u32[]{:S(2)}) collective-permute-start(bf16[60,32,128]{2,1,0:T(8,128)(2,1)} %get-tuple-element.10), channel_id=1, source_target_pairs={{2,0},{4,2},{6,4},{8,6},{10,8},{12,10},{14,12},{16,14},{18,16},{20... | collective-permute-start | bytes 1474568 | tf_op jit(solution)/shard_map/ppermute | solution.py:20
  15.7 0.0 copy-done.2
  15.7 0.1 reshape.26
  15.9 0.2 reshape.32.waves
  16.1 6.4 %table.1 = bf16[2,2,384,1536]{3,2,1,0:T(8,128)(2,1)S(1)} custom-call(s32[2,384,1]{2,1,0:T(8,128)S(1)} %reshape.32.waves), custom_call_target="tpu_custom_call" | custom-call | flops 47185920 | bytes 4718592 | tf_op jit(solution)/shard_map/table/pallas_call | solution.py:116
  22.5 0.0 copy-start
  22.5 2.2 %copy-done = bf16[2,2,384,1536]{3,2,1,0:T(8,128)(2,1)} copy-done((bf16[2,2,384,1536]{3,2,1,0:T(8,128)(2,1)}, bf16[2,2,384,1536]{3,2,1,0:T(8,128)(2,1)S(1)}, u32[]{:S(2)}) %copy-start) | copy-done | bytes 4718616
  24.7 10.4 %collective-permute-done.from_below = bf16[60,32,128]{2,1,0:T(8,128)(2,1)S(1)} collective-permute-done((bf16[60,32,128]{2,1,0:T(8,128)(2,1)}, bf16[60,32,128]{2,1,0:T(8,128)(2,1)S(1)}, u32[]{:S(2)}, u32[]{:S(2)}) %collective-permute-start) | collective-permute-done | bytes 491552 | tf_op jit(solution)/shard_map/ppermute | solution.py:20
  35.1 1.8 %collective-permute-done.1.from_above = bf16[60,32,128]{2,1,0:T(8,128)(2,1)S(1)} collective-permute-done((bf16[60,32,128]{2,1,0:T(8,128)(2,1)}, bf16[60,32,128]{2,1,0:T(8,128)(2,1)S(1)}, u32[]{:S(2)}, u32[]{:S(2)}) %collective-permute-start.1) | collective-permute-done | bytes 491552 | tf_op jit(solution)/shard_map/ppermute | solution.py:20
  36.9 5.9 %fourier.1 = bf16[16,10,24,128]{3,2,1,0:T(8,128)(2,1)S(1)} custom-call(f32[120,32,128]{2,1,0:T(8,128)S(1)} %get-tuple-element.8.mid, bf16[60,32,128]{2,1,0:T(8,128)(2,1)S(1)} %collective-permute-done.from_below, bf16[60,32,128]{2,1,0:T(8,128)(2,1)S(1)} %collective-permute-done.1.from_above, bf16[4,384,1536]{2,1,0:T(8,128)(2,1)} %bitcast.7), custom_call_target="tpu_custom_call" | custom-call | flops 1509949440 | bytes 4718592 | tf_op jit(solution)/shard_map/fourier/pallas_call | solution.py:187
  42.8 29.8 %all_to_all.5 = bf16[16,10,24,128]{3,2,1,0:T(8,128)(2,1)S(1)} all-to-all(bf16[16,10,24,128]{3,2,1,0:T(8,128)(2,1)S(1)} %fourier.1), channel_id=1, replica_groups=mesh['band'=16,'lev'=2] {'band'}, dimensions={0} | all-to-all | bytes 1966080 | tf_op jit(solution)/shard_map/all_to_all | solution.py:303
  72.6 2.7 %collective-permute-start.2 = (bf16[16,10,24,128]{3,2,1,0:T(8,128)(2,1)S(1)}, bf16[16,10,24,128]{3,2,1,0:T(8,128)(2,1)S(1)}, u32[]{:S(2)}, u32[]{:S(2)}) collective-permute-start(bf16[16,10,24,128]{3,2,1,0:T(8,128)(2,1)S(1)} %all_to_all.5), channel_id=1, source_target_pairs={{0,1},{1,0},{2,3},{3,2},{4,5},{5,4},{6,7},{7,6},{8,9},{9,8},{10,11... | collective-permute-start | bytes 2949128 | tf_op jit(solution)/shard_map/ppermute | solution.py:304
  75.3 0.1 dynamic_slice.3.waves
  75.4 2.1 %collective-permute-done.2 = bf16[16,10,24,128]{3,2,1,0:T(8,128)(2,1)S(1)} collective-permute-done((bf16[16,10,24,128]{3,2,1,0:T(8,128)(2,1)S(1)}, bf16[16,10,24,128]{3,2,1,0:T(8,128)(2,1)S(1)}, u32[]{:S(2)}, u32[]{:S(2)}) %collective-permute-start.2) | collective-permute-done | bytes 983072 | tf_op jit(solution)/shard_map/ppermute | solution.py:304
  77.5 9.6 %legendre_sums.1 = bf16[2,24,64,2,384]{4,3,2,1,0:T(2,128)(2,1)} custom-call(s32[48]{0:T(128)S(1)} %dynamic_slice.3.waves, s32[1]{0:T(128)} %bitcast.place, bf16[160,24,128]{2,1,0:T(8,128)(2,1)S(1)} %bitcast.8, bf16[160,24,128]{2,1,0:T(8,128)(2,1)S(1)} %bitcast.9, bf16[48,160,384]{2,1,0:T(8,128)(2,1)} %leg_b.1, bf16[48,160,384]{2,1,0:T(8,128)(2,1)} %leg_b.1), custom_call_target="tpu_custom_call" | custom-call | flops 754974720 | bytes 10616832 | tf_op jit(solution)/shard_map/legendre_sums/pallas_call | solution.py:276
  (3 shorter events, 0.1 us)
Async XLA Ops:
  0.0 15.7 %copy-start.2 = (s32[768]{0:T(1024)S(1)}, s32[768]{0:T(1024)}, u32[]{:S(2)}) copy-start(s32[768]{0:T(1024)} %param.8) | copy-start | bytes 9220
  0.8 1.2 %copy-start.1 = (bf16[10,32,1536]{2,1,0:T(8,128)(2,1)S(1)}, bf16[10,32,1536]{2,1,0:T(8,128)(2,1)}, u32[]{:S(2)}) copy-start(bf16[10,32,1536]{2,1,0:T(8,128)(2,1)} %arrival.1) | copy-start | bytes 2949124
  10.4 24.7 %collective-permute-start = (bf16[60,32,128]{2,1,0:T(8,128)(2,1)}, bf16[60,32,128]{2,1,0:T(8,128)(2,1)S(1)}, u32[]{:S(2)}, u32[]{:S(2)}) collective-permute-start(bf16[60,32,128]{2,1,0:T(8,128)(2,1)} %get-tuple-element.9), channel_id=1, source_target_pairs={{0,2},{2,4},{4,6},{6,8},{8,10},{10,12},{12,14},{14,16},{16,18},{18... | collective-permute-start | bytes 1474568 | tf_op jit(solution)/shard_map/ppermute | solution.py:20
  14.4 22.5 %collective-permute-start.1 = (bf16[60,32,128]{2,1,0:T(8,128)(2,1)}, bf16[60,32,128]{2,1,0:T(8,128)(2,1)S(1)}, u32[]{:S(2)}, u32[]{:S(2)}) collective-permute-start(bf16[60,32,128]{2,1,0:T(8,128)(2,1)} %get-tuple-element.10), channel_id=1, source_target_pairs={{2,0},{4,2},{6,4},{8,6},{10,8},{12,10},{14,12},{16,14},{18,16},{20... | collective-permute-start | bytes 1474568 | tf_op jit(solution)/shard_map/ppermute | solution.py:20
  22.5 2.2 %copy-start = (bf16[2,2,384,1536]{3,2,1,0:T(8,128)(2,1)}, bf16[2,2,384,1536]{3,2,1,0:T(8,128)(2,1)S(1)}, u32[]{:S(2)}) copy-start(bf16[2,2,384,1536]{3,2,1,0:T(8,128)(2,1)S(1)} %table.1) | copy-start | bytes 14155780
  72.6 4.9 %collective-permute-start.2 = (bf16[16,10,24,128]{3,2,1,0:T(8,128)(2,1)S(1)}, bf16[16,10,24,128]{3,2,1,0:T(8,128)(2,1)S(1)}, u32[]{:S(2)}, u32[]{:S(2)}) collective-permute-start(bf16[16,10,24,128]{3,2,1,0:T(8,128)(2,1)S(1)} %all_to_all.5), channel_id=1, source_target_pairs={{0,1},{1,0},{2,3},{3,2},{4,5},{5,4},{6,7},{7,6},{8,9},{9,8},{10,11... | collective-permute-start | bytes 2949128 | tf_op jit(solution)/shard_map/ppermute | solution.py:304

commit v2 on v1

v2 whole, which is shorter than its diff:
```python
import functools
import math

import jax
import jax.numpy as jnp
from jax import lax
from jax.experimental import pallas as pl
from jax.experimental.pallas import tpu as pltpu
from jax.sharding import PartitionSpec as P

BF = jnp.bfloat16
F32 = jnp.float32
LANES = 128
MIB = 2**20
A_LIMIT = 56 * MIB
T_LIMIT = 44 * MIB
VMEM = pl.BlockSpec(memory_space=pltpu.VMEM)
ANY = pl.BlockSpec(memory_space=pl.ANY)


def exchanged(block, pairs):
    return lax.ppermute(block, "band", pairs + [(j, i) for i, j in pairs])


def interpolate_kernel(
    rim, odd, depart, arrival, tiles, first, second, mid, rows, weights, sums, landed
):
    lats, blocks, width = tiles.shape[0], tiles.shape[1], tiles.shape[2]
    whole_rows = pltpu.make_async_copy(arrival, rows, landed.at[0])
    whole_rows.start()
    split = lats // 2
    halves = []
    for i, some in enumerate((slice(0, split), slice(split, lats))):
        halves.append(pltpu.make_async_copy(tiles.at[some], weights.at[some], landed.at[i + 1]))
        halves[i].start()
    sums[...] = jnp.zeros_like(sums)
    whole_rows.wait()
    for lat in range(lats):
        if lat in (0, split):
            halves[lat // split].wait()
        contrib = [
            jnp.dot(
                rows[lat, :, b * width : (b + 1) * width],
                weights[lat, b],
                preferred_element_type=F32,
            )
            for b in range(blocks)
        ]
        for b in range(blocks):
            sums[depart[lat, b]] += contrib[b]
    above = sums.shape[0] - rim
    first[...] = sums[pl.ds(jnp.where(odd[0] == 0, above, 0), rim)].astype(BF)
    second[...] = sums[pl.ds(jnp.where(odd[0] == 0, 0, above), rim)].astype(BF)
    mid[...] = sums[rim:above].astype(BF)


def interpolate(arrival, tiles, depart, odd):
    lats, levels, lons = arrival.shape
    blocks, width = tiles.shape[1], tiles.shape[2]
    rim = lats // 2 * blocks
    segments = lats * blocks + 2 * rim
    grid_spec = pltpu.PrefetchScalarGridSpec(
        num_scalar_prefetch=2,
        grid=(1,),
        in_specs=[ANY, ANY],
        out_specs=[VMEM, VMEM, VMEM],
        scratch_shapes=[
            pltpu.VMEM(arrival.shape, BF),
            pltpu.VMEM(tiles.shape, BF),
            pltpu.VMEM((segments, levels, width), F32),
            pltpu.SemaphoreType.DMA((3,)),
        ],
    )
    return pl.pallas_call(
        functools.partial(interpolate_kernel, rim),
        grid_spec=grid_spec,
        out_shape=[
            jax.ShapeDtypeStruct((rim, levels, width), BF),
            jax.ShapeDtypeStruct((rim, levels, width), BF),
            jax.ShapeDtypeStruct((segments - 2 * rim, levels, width), BF),
        ],
        compiler_params=pltpu.CompilerParams(vmem_limit_bytes=A_LIMIT),
        cost_estimate=pl.CostEstimate(
            flops=2 * lats * levels * lons * width,
            bytes_accessed=2 * (arrival.size + tiles.size),
            transcendentals=0,
        ),
        name="interpolate",
    )(odd, depart, arrival, tiles)


def table_kernel(lons, waves, table):
    blocks = lons // LANES
    rows = waves.shape[1]
    wave = waves[0].astype(F32)
    lane = lax.broadcasted_iota(jnp.int32, (rows, LANES), 1).astype(F32)
    product = lane * wave

    def turn(steps, period):
        left = steps - period * jnp.floor((steps + 0.5) * (1.0 / period))
        angle = left * (2.0 * math.pi / period)
        return jnp.cos(angle), jnp.sin(angle)

    fine_cos, fine_sin = turn(product, float(lons))
    coarse_cos, coarse_sin = turn(product, float(blocks))
    factor = math.sqrt(2.0 / lons)
    coarse_cos = coarse_cos * factor
    coarse_sin = coarse_sin * factor
    for b in range(blocks):
        cos_b, sin_b = coarse_cos[:, b : b + 1], coarse_sin[:, b : b + 1]
        at = slice(b * LANES, (b + 1) * LANES)
        table[0, 0, :, at] = (cos_b * fine_cos - sin_b * fine_sin).astype(BF)
        table[0, 1, :, at] = (sin_b * fine_cos + cos_b * fine_sin).astype(BF)


def wave_table(waves, lons):
    halves, count, _ = waves.shape
    rows = count
    return pl.pallas_call(
        functools.partial(table_kernel, lons),
        grid=(halves, count // rows),
        in_specs=[pl.BlockSpec((1, rows, 1), lambda h, i: (h, i, 0))],
        out_specs=pl.BlockSpec((1, 2, rows, lons), lambda h, i: (h, 0, i, 0)),
        out_shape=jax.ShapeDtypeStruct((halves, 2, count, lons), BF),
        compiler_params=pltpu.CompilerParams(vmem_limit_bytes=20 * MIB),
        cost_estimate=pl.CostEstimate(
            flops=40 * halves * count * lons, bytes_accessed=4 * halves * count * lons, transcendentals=0
        ),
        name="table",
    )(waves)


def fourier_kernel(odd, held, first, second, table, sent, grid, sums):
    levels, width = held.shape[1], held.shape[2]
    rim = first.shape[0]
    bands, lats, half, _ = sent.shape
    blocks = 2 * rim // lats
    per_row = LANES // levels
    parts = table.shape[0]
    groups = pl.cdiv(lats, per_row)

    for lat in range(groups * per_row):
        group, place = lat // per_row, lat % per_row
        for b in range(blocks):
            seg = lat * blocks + b
            if lat >= lats:
                row = jnp.zeros((levels, width), BF)
            else:
                at = seg % rim
                add = jnp.where((odd[0] == 1) == (seg < rim), first[at], second[at])
                row = (held[seg].astype(F32) + add.astype(F32)).astype(BF)
            for k in range(parts):
                start = group * LANES + (place + k) % per_row * levels
                grid[k, start : start + levels, b * width : (b + 1) * width] = row

    for k in range(parts):
        sums[k] = lax.dot_general(
            table[k], grid[k], (((1,), (1,)), ((), ())), preferred_element_type=F32
        )
    index = lax.broadcasted_iota(jnp.int32, (half, LANES), 1)
    lane = index // levels
    part = lane // 2 * 2 + index % 2
    level = index % (2 * levels) // 2
    for d in range(bands):
        for group in range(groups):
            pieces = [
                sums[k, d * half : (d + 1) * half, group * LANES : (group + 1) * LANES]
                for k in range(parts)
            ]
            for place in range(min(per_row, lats - group * per_row)):
                row = pieces[(0 - place) % per_row]
                for p in range(1, per_row):
                    row = jnp.where(lane == p, pieces[(p - place) % per_row], row)
                source = (part + place) % per_row * levels + level
                row = jnp.take_along_axis(row, source, axis=1, mode="promise_in_bounds")
                sent[d, group * per_row + place] = row.astype(BF)


def fourier(odd, held, first, second, table, bands):
    levels, width = held.shape[1], held.shape[2]
    halves, _, count, lons = table.shape
    lats = 2 * first.shape[0] * width // lons
    half = count // bands
    parts = 2 * halves
    groups = pl.cdiv(lats * levels, LANES)
    return pl.pallas_call(
        fourier_kernel,
        in_specs=[pl.BlockSpec(memory_space=pltpu.SMEM)] + [VMEM] * 4,
        out_specs=VMEM,
        out_shape=jax.ShapeDtypeStruct((bands, lats, half, LANES), BF),
        scratch_shapes=[
            pltpu.VMEM((parts, groups * LANES, lons), BF),
            pltpu.VMEM((parts, count, groups * LANES), F32),
        ],
        compiler_params=pltpu.CompilerParams(vmem_limit_bytes=14 * MIB),
        cost_estimate=pl.CostEstimate(
            flops=4 * halves * count * lons * lats * levels,
            bytes_accessed=4 * halves * count * lons,
            transcendentals=0,
        ),
        name="fourier",
    )(odd, held, first, second, table.reshape(parts, count, lons))


def turn_kernel(data, legendre, turned, table, wide, landed):
    lats, half, _ = data.shape
    copy = pltpu.make_async_copy(legendre, table, landed)
    copy.start()
    wide[...] = data[...].astype(F32).reshape(wide.shape)
    for r in range(half):
        turned[r] = wide[pl.ds(r, lats, stride=half), :].T.astype(BF)
    copy.wait()


def turn(data, legendre):
    lats, half, lanes = data.shape
    return pl.pallas_call(
        turn_kernel,
        in_specs=[VMEM, ANY],
        out_specs=[VMEM, VMEM],
        out_shape=[
            jax.ShapeDtypeStruct((half, lanes, lats), BF),
            jax.ShapeDtypeStruct(legendre.shape, BF),
        ],
        scratch_shapes=[pltpu.VMEM((lats * half, lanes), F32), pltpu.SemaphoreType.DMA],
        compiler_params=pltpu.CompilerParams(vmem_limit_bytes=T_LIMIT),
        cost_estimate=pl.CostEstimate(
            flops=0, bytes_accessed=4 * data.size + 2 * legendre.size, transcendentals=0
        ),
        name="turn",
    )(data, legendre)


def legendre_kernel(chunk, waves, lev, own, data, legendre, out, wide, staged, left):
    lats, half, lanes = data.shape
    levels = lanes // 4
    side = lanes // 2
    degrees = legendre.shape[2]
    wide[...] = data[...].astype(F32).reshape(wide.shape)
    column = lax.broadcasted_iota(jnp.int32, (lanes, degrees), 1) + lev[0] * degrees
    places = [lev[0] * levels, (1 - lev[0]) * levels]
    leaving = []
    for c in range(2):
        count = (half + 1 - c) // 2
        first = c * (half - count)

        @pl.loop(0, count // chunk)
        def _(step):
            for i in range(chunk):
                r = first + step * chunk + i
                turned = wide[pl.ds(r, lats, stride=half), :].T.astype(BF)
                for slot in range(2):
                    at = slice(slot * side, (slot + 1) * side)
                    sums = jnp.dot(
                        jnp.concatenate([own[r, at], turned[at]], axis=0),
                        legendre[2 * r + slot],
                        preferred_element_type=F32,
                    )
                    sums = jnp.where(column >= waves[2 * r + slot], sums, 0.0).astype(BF)
                    sums = sums.reshape(2, levels, 2, degrees)
                    for core in range(2):
                        staged[r, slot, pl.ds(places[core], levels)] = sums[core]

        some = slice(first, first + count)
        leaving.append(pltpu.make_async_copy(staged.at[some], out.at[some], left.at[c]))
        leaving[c].start()
    for copy in leaving:
        copy.wait()


def legendre_sums(own, other, legendre, waves, lev):
    slots, lats, degrees = legendre.shape
    half, lanes = slots // 2, other.shape[2]
    levels = lanes // 4
    chunk = 4 if half % 8 == 0 else 1
    grid_spec = pltpu.PrefetchScalarGridSpec(
        num_scalar_prefetch=2,
        grid=(1,),
        in_specs=[VMEM, VMEM, VMEM],
        out_specs=ANY,
        scratch_shapes=[
            pltpu.VMEM((lats * half, lanes), F32),
            pltpu.VMEM((half, 2, 2 * levels, 2, degrees), BF),
            pltpu.SemaphoreType.DMA((2,)),
        ],
    )
    return pl.pallas_call(
        functools.partial(legendre_kernel, chunk),
        grid_spec=grid_spec,
        out_shape=jax.ShapeDtypeStruct((half, 2, 2 * levels, 2, degrees), BF),
        compiler_params=pltpu.CompilerParams(vmem_limit_bytes=18 * MIB),
        cost_estimate=pl.CostEstimate(
            flops=2 * slots * lats * lanes * degrees,
            bytes_accessed=2 * slots * lanes * degrees,
            transcendentals=0,
        ),
        name="legendre_sums",
    )(waves, lev, own, other, legendre)


def local(arrival_adjoint, interp_tiles, departure_block, slot_wavenumber, legendre):
    lons = arrival_adjoint.shape[2]
    slots = legendre.shape[0]
    bands = lax.axis_size("band")
    lev = lax.axis_index("lev")
    odd = (lax.axis_index("band") % 2).reshape(1)
    first, second, held = interpolate(arrival_adjoint, interp_tiles, departure_block, odd)
    second = exchanged(second, [(i, i + 1) for i in range(1, bands - 1, 2)])
    first = exchanged(first, [(i, i + 1) for i in range(0, bands - 1, 2)])
    table = wave_table(slot_wavenumber.reshape(-1, 2).T[:, :, None], lons)
    sent = fourier(odd, held, first, second, table, bands)
    own = lax.all_to_all(sent, "band", split_axis=0, concat_axis=0)
    own = own.reshape(-1, *own.shape[2:])
    other = lax.ppermute(own, "lev", [(0, 1), (1, 0)])
    waves = lax.dynamic_slice_in_dim(slot_wavenumber, lax.axis_index("band") * slots, slots)
    own, legendre = turn(own, legendre)
    done = legendre_sums(own, other, legendre, waves, lev.reshape(1))
    return done.reshape(slots, done.shape[2], 2, done.shape[4])


def solution(mesh):
    placed = (
        P("band", "lev", None),
        P("band", None, None, None),
        P("band", None),
        P(),
        P("band", None, "lev"),
    )
    return jax.shard_map(
        local, mesh=mesh, in_specs=placed, out_specs=P("band", None, None, "lev"), check_vma=False
    )
```

time: 88 us -> 73.3 us (0.83)
  Pallas kernels: 30.4 us -> 22.4 us
  waiting for transfers between devices: 14.4 us -> 11.6 us
  starting transfers between devices: 7.91 us -> 5.7 us
  local copies, waits for them, and re-layouts: 4.55 us -> 2.79 us
    pallas_call x2 -> x3, Pallas kernels: 15.5 us -> 11.3 us  [the longest x1 5.08 us: legendre_sums(): pl.pallas_call(functools.partial(legendre_kernel, chunk), grid_spec=grid_...]
    unnamed x6 -> x4, local copies, waits for them, and re-layouts: 3.39 us -> 0.01 us
    pallas_call x1, Pallas kernels: 8.44 us -> 5.38 us  [interpolate(): pl.pallas_call(functools.partial(interpolate_kernel, rim), grid_spec=grid...]
    broadcast_in_dim x0 -> x1, local copies, waits for them, and re-layouts: none -> 2.55 us  [local(): table = wave_table(slot_wavenumber.reshape(-1, 2).T[:, :, None], lons)]
    ppermute x2, starting transfers between devices: 5.25 us -> 2.79 us  [exchanged(): return lax.ppermute(block, 'band', pairs + [(j, i) for i, j in pairs])]
    ppermute x1, waiting for transfers between devices: 2.12 us -> 0.01 us  [local(): other = lax.ppermute(own, 'lev', [(0, 1), (1, 0)])]
  transfers between devices with their start and end apart: 3 -> 3, of which waited for: 3 -> 1; matrix products, arithmetic and copies ran while one was open for 0% -> 4% of each run, Pallas kernels for 7% -> 11%
where the time goes in v2:
time: 73.3 us; the launch traced here: 73.1 us
  blocking collectives  30.5 us (42%)
  Pallas kernels  22.4 us (31%)
  waiting for transfers between devices  11.6 us (16%)
  starting transfers between devices  5.7 us (8%)
  local copies, waits for them, and re-layouts  2.79 us (4%)
    all_to_all x1, blocking collectives, local(): own = lax.all_to_all(sent, 'band', split_axis=0, concat_axis=0)  30.5 us
    ppermute x2, waiting for transfers between devices, exchanged(): return lax.ppermute(block, 'band', pairs + [(j, i) for i, j in pairs])  11.6 us
    pallas_call x1, Pallas kernels, wave_table(): pl.pallas_call(functools.partial(table_kernel, lons), grid=(halves, count...  5.69 us
    pallas_call x1, Pallas kernels, interpolate(): pl.pallas_call(functools.partial(interpolate_kernel, rim), grid_spec=grid...  5.38 us
    pallas_call x1, Pallas kernels, legendre_sums(): pl.pallas_call(functools.partial(legendre_kernel, chunk), grid_spec=grid_...  5.08 us
    pallas_call x1, Pallas kernels, fourier(): pl.pallas_call(fourier_kernel, in_specs=[pl.BlockSpec(memory_space=pltpu....  3.59 us
    ppermute x1, starting transfers between devices, local(): other = lax.ppermute(own, 'lev', [(0, 1), (1, 0)])  2.91 us
    ppermute x2, starting transfers between devices, exchanged(): return lax.ppermute(block, 'band', pairs + [(j, i) for i, j in pairs])  2.79 us
  transfers between devices with their start and end apart: 3, of which 1 were waited for; matrix products, arithmetic and copies ran while one was open for 4% of the time, Pallas kernels for 11%

profile of v2, /device:TPU:1, one launch (start us, length us, event | category | flops | bytes accessed | tf_op | source)
XLA Modules:
  0.0 73.1 jit_solution(2858572220837590687)
XLA Ops:
  0.0 0.0 copy-start.1
  0.0 5.4 %interpolate.1 = (bf16[60,32,128]{2,1,0:T(8,128)(2,1)}, bf16[60,32,128]{2,1,0:T(8,128)(2,1)}, bf16[120,32,128]{2,1,0:T(8,128)(2,1)}) custom-call(s32[1]{0:T(128)} %bitcast.1.odd, s32[10,12]{1,0:T(8,128)} %depart.1, bf16[10,32,1536]{2,1,0:T(8,128)(2,1)} %arrival.1, bf16[10,12,128,128]{3,2,1,0:T(8,128)(2,1)} %tiles.1), custom_call_target="tpu_custom_call" | custom-call | flops 125829120 | bytes 4915200 | tf_op jit(solution)/shard_map/interpolate/pallas_call | solution.py:74
  5.4 0.0 copy-start
  5.4 2.1 %collective-permute-start = (bf16[60,32,128]{2,1,0:T(8,128)(2,1)}, bf16[60,32,128]{2,1,0:T(8,128)(2,1)S(1)}, u32[]{:S(2)}, u32[]{:S(2)}) collective-permute-start(bf16[60,32,128]{2,1,0:T(8,128)(2,1)} %get-tuple-element.11), channel_id=1, source_target_pairs={{0,2},{4,6},{8,10},{12,14},{16,18},{20,22},{24,26},{28,30},{2,0},{... | collective-permute-start | bytes 1474568 | tf_op jit(solution)/shard_map/ppermute | solution.py:22
  7.5 0.7 collective-permute-start.1
  8.2 0.0 copy-done.1
  8.2 0.2 reshape.20
  8.4 2.5 %copy.7.waves = s32[2,384,1]{2,1,0:T(8,128)S(1)} copy(s32[2,384,1]{0,1,2:T(8,128)S(1)} %bitcast.11) | data formatting | bytes 6144 | tf_op jit(solution)/shard_map/broadcast_in_dim | solution.py:310
  10.9 5.7 %table.1 = bf16[2,2,384,1536]{3,2,1,0:T(8,128)(2,1)S(1)} custom-call(s32[2,384,1]{2,1,0:T(8,128)S(1)} %copy.7.waves), custom_call_target="tpu_custom_call" | custom-call | flops 47185920 | bytes 4718592 | tf_op jit(solution)/shard_map/table/pallas_call | solution.py:119
  16.6 11.6 %collective-permute-done.first = bf16[60,32,128]{2,1,0:T(8,128)(2,1)S(1)} collective-permute-done((bf16[60,32,128]{2,1,0:T(8,128)(2,1)}, bf16[60,32,128]{2,1,0:T(8,128)(2,1)S(1)}, u32[]{:S(2)}, u32[]{:S(2)}) %collective-permute-start) | collective-permute-done | bytes 491552 | tf_op jit(solution)/shard_map/ppermute | solution.py:22
  28.2 0.0 collective-permute-done.1.second
  28.2 0.0 copy-done
  28.2 3.6 %fourier.1 = bf16[16,10,24,128]{3,2,1,0:T(8,128)(2,1)S(1)} custom-call(s32[1]{0:T(128)} %bitcast.1.odd, bf16[120,32,128]{2,1,0:T(8,128)(2,1)S(1)} %copy-done, bf16[60,32,128]{2,1,0:T(8,128)(2,1)S(1)} %collective-permute-done.first, bf16[60,32,128]{2,1,0:T(8,128)(2,1)S(1)} %collective-permute-done.1.second, bf16[4,384,1536]{2,1,0:T(8,128)(2,1)S(1)} %bitcast.8), custom_call_target="tpu_custom_call" | custom-call | flops 1509949440 | bytes 4718592 | tf_op jit(solution)/shard_map/fourier/pallas_call | solution.py:186
  31.8 30.5 %all_to_all.5 = bf16[16,10,24,128]{3,2,1,0:T(8,128)(2,1)S(1)} all-to-all(bf16[16,10,24,128]{3,2,1,0:T(8,128)(2,1)S(1)} %fourier.1), channel_id=1, replica_groups=mesh['band'=16,'lev'=2] {'band'}, dimensions={0} | all-to-all | bytes 1966080 | tf_op jit(solution)/shard_map/all_to_all | solution.py:312
  62.3 2.9 %collective-permute-start.2 = (bf16[160,24,128]{2,1,0:T(8,128)(2,1)S(1)}, bf16[160,24,128]{2,1,0:T(8,128)(2,1)S(1)}, u32[]{:S(2)}, u32[]{:S(2)}) collective-permute-start(bf16[160,24,128]{2,1,0:T(8,128)(2,1)S(1)} %bitcast.9), channel_id=1, source_target_pairs={{0,1},{1,0},{2,3},{3,2},{4,5},{5,4},{6,7},{7,6},{8,9},{9,8},{10,11... | collective-permute-start | bytes 2949128 | tf_op jit(solution)/shard_map/ppermute | solution.py:314
  65.2 0.1 dynamic_slice.3.waves
  65.3 2.7 %turn.1 = (bf16[24,128,160]{2,1,0:T(8,128)(2,1)S(1)}, bf16[48,160,384]{2,1,0:T(8,128)(2,1)S(1)}) custom-call(bf16[160,24,128]{2,1,0:T(8,128)(2,1)S(1)} %bitcast.10, bf16[48,160,384]{2,1,0:T(8,128)(2,1)} %legendre.1), custom_call_target="tpu_custom_call" | custom-call | bytes 7864320 | tf_op jit(solution)/shard_map/turn/pallas_call | solution.py:217
  68.0 0.0 collective-permute-done.2.data
  68.0 5.1 %legendre_sums.1 = bf16[24,2,64,2,384]{4,3,2,1,0:T(2,128)(2,1)} custom-call(s32[48]{0:T(128)S(1)} %dynamic_slice.3.waves, s32[1]{0:T(128)} %bitcast.lev, bf16[24,128,160]{2,1,0:T(8,128)(2,1)S(1)} %get-tuple-element.13.own, bf16[160,24,128]{2,1,0:T(8,128)(2,1)S(1)} %collective-permute-done.2.data, bf16[48,160,384]{2,1,0:T(8,128)(2,1)S(1)} %get-tuple-element.14.legendre), custom_call_target="tpu_custom_call" | custom-call | flops 754974720 | bytes 4718592 | tf_op jit(solution)/shard_map/legendre_sums/pallas_call | solution.py:287
Async XLA Ops:
  0.0 8.2 %copy-start.1 = (s32[768]{0:T(1024)S(1)}, s32[768]{0:T(1024)}, u32[]{:S(2)}) copy-start(s32[768]{0:T(1024)} %param.8) | copy-start | bytes 9220
  5.4 22.9 %copy-start = (bf16[120,32,128]{2,1,0:T(8,128)(2,1)S(1)}, bf16[120,32,128]{2,1,0:T(8,128)(2,1)}, u32[]{:S(2)}) copy-start(bf16[120,32,128]{2,1,0:T(8,128)(2,1)} %get-tuple-element.10.held) | copy-start | bytes 2949124
  5.4 22.8 %collective-permute-start = (bf16[60,32,128]{2,1,0:T(8,128)(2,1)}, bf16[60,32,128]{2,1,0:T(8,128)(2,1)S(1)}, u32[]{:S(2)}, u32[]{:S(2)}) collective-permute-start(bf16[60,32,128]{2,1,0:T(8,128)(2,1)} %get-tuple-element.11), channel_id=1, source_target_pairs={{0,2},{4,6},{8,10},{12,14},{16,18},{20,22},{24,26},{28,30},{2,0},{... | collective-permute-start | bytes 1474568 | tf_op jit(solution)/shard_map/ppermute | solution.py:22
  7.5 20.7 %collective-permute-start.1 = (bf16[60,32,128]{2,1,0:T(8,128)(2,1)}, bf16[60,32,128]{2,1,0:T(8,128)(2,1)S(1)}, u32[]{:S(2)}, u32[]{:S(2)}) collective-permute-start(bf16[60,32,128]{2,1,0:T(8,128)(2,1)} %get-tuple-element.12), channel_id=1, source_target_pairs={{2,4},{6,8},{10,12},{14,16},{18,20},{22,24},{26,28},{4,2},{8,6},{1... | collective-permute-start | bytes 1474568 | tf_op jit(solution)/shard_map/ppermute | solution.py:22
  62.3 5.7 %collective-permute-start.2 = (bf16[160,24,128]{2,1,0:T(8,128)(2,1)S(1)}, bf16[160,24,128]{2,1,0:T(8,128)(2,1)S(1)}, u32[]{:S(2)}, u32[]{:S(2)}) collective-permute-start(bf16[160,24,128]{2,1,0:T(8,128)(2,1)S(1)} %bitcast.9), channel_id=1, source_target_pairs={{0,1},{1,0},{2,3},{3,2},{4,5},{5,4},{6,7},{7,6},{8,9},{9,8},{10,11... | collective-permute-start | bytes 2949128 | tf_op jit(solution)/shard_map/ppermute | solution.py:314

commit v3 on v2

--- a/solution.py
+++ b/solution.py
@@ -23,61 +23,64 @@
 
 
 def interpolate_kernel(
-    rim, odd, depart, arrival, tiles, first, second, mid, rows, weights, sums, landed
+    rim, depart, arrival, tiles, first, second, mid, rows, weights, sums, targets, landed
 ):
     lats, blocks, width = tiles.shape[0], tiles.shape[1], tiles.shape[2]
-    whole_rows = pltpu.make_async_copy(arrival, rows, landed.at[0])
-    whole_rows.start()
-    split = lats // 2
-    halves = []
-    for i, some in enumerate((slice(0, split), slice(split, lats))):
-        halves.append(pltpu.make_async_copy(tiles.at[some], weights.at[some], landed.at[i + 1]))
-        halves[i].start()
+    cuts = [lats * i // 3 for i in range(4)]
+    arriving = [
+        pltpu.make_async_copy(depart, targets, landed.at[0]),
+        pltpu.make_async_copy(arrival, rows, landed.at[1]),
+    ]
+    for i in range(3):
+        some = slice(cuts[i], cuts[i + 1])
+        arriving.append(
+            pltpu.make_async_copy(tiles.at[some], weights.at[some], landed.at[i + 2])
+        )
+    for copy in arriving:
+        copy.start()
     sums[...] = jnp.zeros_like(sums)
-    whole_rows.wait()
-    for lat in range(lats):
-        if lat in (0, split):
-            halves[lat // split].wait()
-        contrib = [
-            jnp.dot(
-                rows[lat, :, b * width : (b + 1) * width],
-                weights[lat, b],
-                preferred_element_type=F32,
-            )
-            for b in range(blocks)
-        ]
-        for b in range(blocks):
-            sums[depart[lat, b]] += contrib[b]
+    arriving[0].wait()
+    arriving[1].wait()
+    for i in range(3):
+        arriving[i + 2].wait()
+        for lat in range(cuts[i], cuts[i + 1]):
+            contrib = [
+                jnp.dot(
+                    rows[lat, :, b * width : (b + 1) * width],
+                    weights[lat, b],
+                    preferred_element_type=F32,
+                )
+                for b in range(blocks)
+            ]
+            for b in range(blocks):
+                sums[targets[lat, b]] += contrib[b]
     above = sums.shape[0] - rim
-    first[...] = sums[pl.ds(jnp.where(odd[0] == 0, above, 0), rim)].astype(BF)
-    second[...] = sums[pl.ds(jnp.where(odd[0] == 0, 0, above), rim)].astype(BF)
+    odd = lax.axis_index("band") % 2
+    first[...] = sums[pl.ds(jnp.where(odd == 0, above, 0), rim)].astype(BF)
+    second[...] = sums[pl.ds(jnp.where(odd == 0, 0, above), rim)].astype(BF)
     mid[...] = sums[rim:above].astype(BF)
 
 
-def interpolate(arrival, tiles, depart, odd):
+def interpolate(arrival, tiles, depart):
     lats, levels, lons = arrival.shape
     blocks, width = tiles.shape[1], tiles.shape[2]
     rim = lats // 2 * blocks
     segments = lats * blocks + 2 * rim
-    grid_spec = pltpu.PrefetchScalarGridSpec(
-        num_scalar_prefetch=2,
-        grid=(1,),
-        in_specs=[ANY, ANY],
+    return pl.pallas_call(
+        functools.partial(interpolate_kernel, rim),
+        in_specs=[ANY, ANY, ANY],
         out_specs=[VMEM, VMEM, VMEM],
+        out_shape=[
+            jax.ShapeDtypeStruct((rim, levels, width), BF),
+            jax.ShapeDtypeStruct((rim, levels, width), BF),
+            jax.ShapeDtypeStruct((segments - 2 * rim, levels, width), BF),
+        ],
         scratch_shapes=[
             pltpu.VMEM(arrival.shape, BF),
             pltpu.VMEM(tiles.shape, BF),
             pltpu.VMEM((segments, levels, width), F32),
-            pltpu.SemaphoreType.DMA((3,)),
-        ],
-    )
-    return pl.pallas_call(
-        functools.partial(interpolate_kernel, rim),
-        grid_spec=grid_spec,
-        out_shape=[
-            jax.ShapeDtypeStruct((rim, levels, width), BF),
-            jax.ShapeDtypeStruct((rim, levels, width), BF),
-            jax.ShapeDtypeStruct((segments - 2 * rim, levels, width), BF),
+            pltpu.SMEM(depart.shape, jnp.int32),
+            pltpu.SemaphoreType.DMA((5,)),
         ],
         compiler_params=pltpu.CompilerParams(vmem_limit_bytes=A_LIMIT),
         cost_estimate=pl.CostEstimate(
@@ -86,7 +89,7 @@
             transcendentals=0,
         ),
         name="interpolate",
-    )(odd, depart, arrival, tiles)
+    )(depart, arrival, tiles)
 
 
 def table_kernel(lons, waves, table):
@@ -130,10 +133,11 @@
     )(waves)
 
 
-def fourier_kernel(odd, held, first, second, table, sent, grid, sums):
+def fourier_kernel(held, first, second, table, sent, grid, sums):
     levels, width = held.shape[1], held.shape[2]
     rim = first.shape[0]
     bands, lats, half, _ = sent.shape
+    odd = lax.axis_index("band") % 2
     blocks = 2 * rim // lats
     per_row = LANES // levels
     parts = table.shape[0]
@@ -147,7 +151,7 @@
                 row = jnp.zeros((levels, width), BF)
             else:
                 at = seg % rim
-                add = jnp.where((odd[0] == 1) == (seg < rim), first[at], second[at])
+                add = jnp.where((odd == 1) == (seg < rim), first[at], second[at])
                 row = (held[seg].astype(F32) + add.astype(F32)).astype(BF)
             for k in range(parts):
                 start = group * LANES + (place + k) % per_row * levels
@@ -176,7 +180,7 @@
                 sent[d, group * per_row + place] = row.astype(BF)
 
 
-def fourier(odd, held, first, second, table, bands):
+def fourier(held, first, second, table, bands):
     levels, width = held.shape[1], held.shape[2]
     halves, _, count, lons = table.shape
     lats = 2 * first.shape[0] * width // lons
@@ -185,7 +189,7 @@
     groups = pl.cdiv(lats * levels, LANES)
     return pl.pallas_call(
         fourier_kernel,
-        in_specs=[pl.BlockSpec(memory_space=pltpu.SMEM)] + [VMEM] * 4,
+        in_specs=[VMEM] * 4,
         out_specs=VMEM,
         out_shape=jax.ShapeDtypeStruct((bands, lats, half, LANES), BF),
         scratch_shapes=[
@@ -199,7 +203,7 @@
             transcendentals=0,
         ),
         name="fourier",
-    )(odd, held, first, second, table.reshape(parts, count, lons))
+    )(held, first, second, table.reshape(parts, count, lons))
 
 
 def turn_kernel(data, legendre, turned, table, wide, landed):
@@ -231,63 +235,58 @@
     )(data, legendre)
 
 
-def legendre_kernel(chunk, waves, lev, own, data, legendre, out, wide, staged, left):
+def legendre_kernel(waves, own, data, legendre, out, wide, staged, wave, landed, left):
     lats, half, lanes = data.shape
     levels = lanes // 4
     side = lanes // 2
     degrees = legendre.shape[2]
+    arriving = pltpu.make_async_copy(waves, wave, landed)
+    arriving.start()
     wide[...] = data[...].astype(F32).reshape(wide.shape)
-    column = lax.broadcasted_iota(jnp.int32, (lanes, degrees), 1) + lev[0] * degrees
-    places = [lev[0] * levels, (1 - lev[0]) * levels]
+    lev = lax.axis_index("lev")
+    owned = lax.axis_index("band") * 2 * half
+    column = lax.broadcasted_iota(jnp.int32, (lanes, degrees), 1) + lev * degrees
+    places = [lev * levels, (1 - lev) * levels]
+    arriving.wait()
     leaving = []
-    for c in range(2):
-        count = (half + 1 - c) // 2
-        first = c * (half - count)
-
-        @pl.loop(0, count // chunk)
-        def _(step):
-            for i in range(chunk):
-                r = first + step * chunk + i
-                turned = wide[pl.ds(r, lats, stride=half), :].T.astype(BF)
-                for slot in range(2):
-                    at = slice(slot * side, (slot + 1) * side)
-                    sums = jnp.dot(
-                        jnp.concatenate([own[r, at], turned[at]], axis=0),
-                        legendre[2 * r + slot],
-                        preferred_element_type=F32,
-                    )
-                    sums = jnp.where(column >= waves[2 * r + slot], sums, 0.0).astype(BF)
-                    sums = sums.reshape(2, levels, 2, degrees)
-                    for core in range(2):
-                        staged[r, slot, pl.ds(places[core], levels)] = sums[core]
-
-        some = slice(first, first + count)
+    count = half // left.shape[0]
+    for c in range(left.shape[0]):
+        for r in range(c * count, (c + 1) * count):
+            turned = wide[pl.ds(r, lats, stride=half), :].T.astype(BF)
+            for slot in range(2):
+                at = slice(slot * side, (slot + 1) * side)
+                sums = jnp.dot(
+                    jnp.concatenate([own[r, at], turned[at]], axis=0),
+                    legendre[2 * r + slot],
+                    preferred_element_type=F32,
+                )
+                keep = column >= wave[owned + 2 * r + slot]
+                sums = jnp.where(keep, sums, 0.0).astype(BF).reshape(2, levels, 2, degrees)
+                for core in range(2):
+                    staged[r, slot, pl.ds(places[core], levels)] = sums[core]
+        some = slice(c * count, (c + 1) * count)
         leaving.append(pltpu.make_async_copy(staged.at[some], out.at[some], left.at[c]))
         leaving[c].start()
     for copy in leaving:
         copy.wait()
 
 
-def legendre_sums(own, other, legendre, waves, lev):
+def legendre_sums(own, other, legendre, waves):
     slots, lats, degrees = legendre.shape
     half, lanes = slots // 2, other.shape[2]
     levels = lanes // 4
-    chunk = 4 if half % 8 == 0 else 1
-    grid_spec = pltpu.PrefetchScalarGridSpec(
-        num_scalar_prefetch=2,
-        grid=(1,),
-        in_specs=[VMEM, VMEM, VMEM],
+    return pl.pallas_call(
+        legendre_kernel,
+        in_specs=[ANY, VMEM, VMEM, VMEM],
         out_specs=ANY,
+        out_shape=jax.ShapeDtypeStruct((half, 2, 2 * levels, 2, degrees), BF),
         scratch_shapes=[
             pltpu.VMEM((lats * half, lanes), F32),
             pltpu.VMEM((half, 2, 2 * levels, 2, degrees), BF),
-            pltpu.SemaphoreType.DMA((2,)),
-        ],
-    )
-    return pl.pallas_call(
-        functools.partial(legendre_kernel, chunk),
-        grid_spec=grid_spec,
-        out_shape=jax.ShapeDtypeStruct((half, 2, 2 * levels, 2, degrees), BF),
+            pltpu.SMEM(waves.shape, jnp.int32),
+            pltpu.SemaphoreType.DMA,
+            pltpu.SemaphoreType.DMA((math.gcd(half, 6),)),
+        ],
         compiler_params=pltpu.CompilerParams(vmem_limit_bytes=18 * MIB),
         cost_estimate=pl.CostEstimate(
             flops=2 * slots * lats * lanes * degrees,
@@ -295,26 +294,23 @@
             transcendentals=0,
         ),
         name="legendre_sums",
-    )(waves, lev, own, other, legendre)
+    )(waves, own, other, legendre)
 
 
 def local(arrival_adjoint, interp_tiles, departure_block, slot_wavenumber, legendre):
     lons = arrival_adjoint.shape[2]
     slots = legendre.shape[0]
     bands = lax.axis_size("band")
-    lev = lax.axis_index("lev")
-    odd = (lax.axis_index("band") % 2).reshape(1)
-    first, second, held = interpolate(arrival_adjoint, interp_tiles, departure_block, odd)
+    first, second, held = interpolate(arrival_adjoint, interp_tiles, departure_block)
     second = exchanged(second, [(i, i + 1) for i in range(1, bands - 1, 2)])
     first = exchanged(first, [(i, i + 1) for i in range(0, bands - 1, 2)])
     table = wave_table(slot_wavenumber.reshape(-1, 2).T[:, :, None], lons)
-    sent = fourier(odd, held, first, second, table, bands)
+    sent = fourier(held, first, second, table, bands)
     own = lax.all_to_all(sent, "band", split_axis=0, concat_axis=0)
     own = own.reshape(-1, *own.shape[2:])
     other = lax.ppermute(own, "lev", [(0, 1), (1, 0)])
-    waves = lax.dynamic_slice_in_dim(slot_wavenumber, lax.axis_index("band") * slots, slots)
     own, legendre = turn(own, legendre)
-    done = legendre_sums(own, other, legendre, waves, lev.reshape(1))
+    done = legendre_sums(own, other, legendre, slot_wavenumber)
     return done.reshape(slots, done.shape[2], 2, done.shape[4])
 
 

time: 73.3 us -> 70.5 us (0.962)
  Pallas kernels: 22.4 us -> 19.8 us
    pallas_call x3, Pallas kernels: 14 us -> 11.4 us  [the longest x1 4.32 us: interpolate(): pl.pallas_call(functools.partial(interpolate_kernel, rim), in_specs=[ANY,...]
  transfers between devices with their start and end apart: 3 -> 3, of which waited for: 1 -> 1; matrix products, arithmetic and copies ran while one was open for 4% -> 4% of each run, Pallas kernels for 11% -> 12%
where the time goes in v3:
time: 70.5 us; the launch traced here: 70.3 us
  blocking collectives  30.5 us (43%)
  Pallas kernels  19.8 us (28%)
  waiting for transfers between devices  11.6 us (16%)
  starting transfers between devices  5.7 us (8%)
  local copies, waits for them, and re-layouts  2.72 us (4%)
    all_to_all x1, blocking collectives, local(): own = lax.all_to_all(sent, 'band', split_axis=0, concat_axis=0)  30.5 us
    ppermute x2, waiting for transfers between devices, exchanged(): return lax.ppermute(block, 'band', pairs + [(j, i) for i, j in pairs])  11.6 us
    pallas_call x1, Pallas kernels, wave_table(): pl.pallas_call(functools.partial(table_kernel, lons), grid=(halves, count...  5.69 us
    pallas_call x1, Pallas kernels, interpolate(): pl.pallas_call(functools.partial(interpolate_kernel, rim), in_specs=[ANY,...  4.32 us
    pallas_call x1, Pallas kernels, legendre_sums(): pl.pallas_call(legendre_kernel, in_specs=[ANY, VMEM, VMEM, VMEM], out_spe...  3.55 us
    pallas_call x1, Pallas kernels, fourier(): pl.pallas_call(fourier_kernel, in_specs=[VMEM] * 4, out_specs=VMEM, out_s...  3.51 us
    ppermute x1, starting transfers between devices, local(): other = lax.ppermute(own, 'lev', [(0, 1), (1, 0)])  2.91 us
    ppermute x2, starting transfers between devices, exchanged(): return lax.ppermute(block, 'band', pairs + [(j, i) for i, j in pairs])  2.79 us
  transfers between devices with their start and end apart: 3, of which 1 were waited for; matrix products, arithmetic and copies ran while one was open for 4% of the time, Pallas kernels for 12%

profile of v3, /device:TPU:1, one launch (start us, length us, event | category | flops | bytes accessed | tf_op | source)
XLA Modules:
  0.0 70.3 jit_solution(3822488832017713175)
XLA Ops:
  0.0 0.0 copy-start.1
  0.0 4.3 %interpolate.1 = (bf16[60,32,128]{2,1,0:T(8,128)(2,1)}, bf16[60,32,128]{2,1,0:T(8,128)(2,1)}, bf16[120,32,128]{2,1,0:T(8,128)(2,1)}) custom-call(s32[10,12]{1,0:T(8,128)} %depart.1, bf16[10,32,1536]{2,1,0:T(8,128)(2,1)} %arrival.1, bf16[10,12,128,128]{3,2,1,0:T(8,128)(2,1)} %tiles.1), custom_call_target="tpu_custom_call" | custom-call | flops 125829120 | bytes 4915200 | tf_op jit(solution)/shard_map/interpolate/pallas_call | solution.py:69
  4.3 0.0 copy-start
  4.3 2.1 %collective-permute-start = (bf16[60,32,128]{2,1,0:T(8,128)(2,1)}, bf16[60,32,128]{2,1,0:T(8,128)(2,1)S(1)}, u32[]{:S(2)}, u32[]{:S(2)}) collective-permute-start(bf16[60,32,128]{2,1,0:T(8,128)(2,1)} %get-tuple-element.11), channel_id=1, source_target_pairs={{0,2},{4,6},{8,10},{12,14},{16,18},{20,22},{24,26},{28,30},{2,0},{... | collective-permute-start | bytes 1474568 | tf_op jit(solution)/shard_map/ppermute | solution.py:22
  6.4 0.7 collective-permute-start.1
  7.1 0.0 copy-done.1
  7.1 0.2 reshape.12
  7.3 2.5 %copy.7.waves = s32[2,384,1]{2,1,0:T(8,128)S(1)} copy(s32[2,384,1]{0,1,2:T(8,128)S(1)} %bitcast.9) | data formatting | bytes 6144 | tf_op jit(solution)/shard_map/broadcast_in_dim | solution.py:307
  9.9 5.7 %table.1 = bf16[2,2,384,1536]{3,2,1,0:T(8,128)(2,1)S(1)} custom-call(s32[2,384,1]{2,1,0:T(8,128)S(1)} %copy.7.waves), custom_call_target="tpu_custom_call" | custom-call | flops 47185920 | bytes 4718592 | tf_op jit(solution)/shard_map/table/pallas_call | solution.py:122
  15.6 11.6 %collective-permute-done.first = bf16[60,32,128]{2,1,0:T(8,128)(2,1)S(1)} collective-permute-done((bf16[60,32,128]{2,1,0:T(8,128)(2,1)}, bf16[60,32,128]{2,1,0:T(8,128)(2,1)S(1)}, u32[]{:S(2)}, u32[]{:S(2)}) %collective-permute-start) | collective-permute-done | bytes 491552 | tf_op jit(solution)/shard_map/ppermute | solution.py:22
  27.2 0.0 collective-permute-done.1.second
  27.2 0.0 copy-done
  27.2 3.5 %fourier.1 = bf16[16,10,24,128]{3,2,1,0:T(8,128)(2,1)S(1)} custom-call(bf16[120,32,128]{2,1,0:T(8,128)(2,1)S(1)} %copy-done, bf16[60,32,128]{2,1,0:T(8,128)(2,1)S(1)} %collective-permute-done.first, bf16[60,32,128]{2,1,0:T(8,128)(2,1)S(1)} %collective-permute-done.1.second, bf16[4,384,1536]{2,1,0:T(8,128)(2,1)S(1)} %bitcast.6), custom_call_target="tpu_custom_call" | custom-call | flops 1509949440 | bytes 4718592 | tf_op jit(solution)/shard_map/fourier/pallas_call | solution.py:190
  30.7 30.5 %all_to_all.5 = bf16[16,10,24,128]{3,2,1,0:T(8,128)(2,1)S(1)} all-to-all(bf16[16,10,24,128]{3,2,1,0:T(8,128)(2,1)S(1)} %fourier.1), channel_id=1, replica_groups=mesh['band'=16,'lev'=2] {'band'}, dimensions={0} | all-to-all | bytes 1966080 | tf_op jit(solution)/shard_map/all_to_all | solution.py:309
  61.2 2.9 %collective-permute-start.2 = (bf16[160,24,128]{2,1,0:T(8,128)(2,1)S(1)}, bf16[160,24,128]{2,1,0:T(8,128)(2,1)S(1)}, u32[]{:S(2)}, u32[]{:S(2)}) collective-permute-start(bf16[160,24,128]{2,1,0:T(8,128)(2,1)S(1)} %bitcast.7), channel_id=1, source_target_pairs={{0,1},{1,0},{2,3},{3,2},{4,5},{5,4},{6,7},{7,6},{8,9},{9,8},{10,11... | collective-permute-start | bytes 2949128 | tf_op jit(solution)/shard_map/ppermute | solution.py:311
  64.1 2.7 %turn.1 = (bf16[24,128,160]{2,1,0:T(8,128)(2,1)S(1)}, bf16[48,160,384]{2,1,0:T(8,128)(2,1)S(1)}) custom-call(bf16[160,24,128]{2,1,0:T(8,128)(2,1)S(1)} %bitcast.8, bf16[48,160,384]{2,1,0:T(8,128)(2,1)} %legendre.1), custom_call_target="tpu_custom_call" | custom-call | bytes 7864320 | tf_op jit(solution)/shard_map/turn/pallas_call | solution.py:221
  66.8 0.0 collective-permute-done.2.data
  66.8 3.5 %legendre_sums.1 = bf16[24,2,64,2,384]{4,3,2,1,0:T(2,128)(2,1)} custom-call(s32[768]{0:T(1024)S(1)} %copy-done.1, bf16[24,128,160]{2,1,0:T(8,128)(2,1)S(1)} %get-tuple-element.13.own, bf16[160,24,128]{2,1,0:T(8,128)(2,1)S(1)} %collective-permute-done.2.data, bf16[48,160,384]{2,1,0:T(8,128)(2,1)S(1)} %get-tuple-element.14.legendre), custom_call_target="tpu_custom_call" | custom-call | flops 754974720 | bytes 4718592 | tf_op jit(solution)/shard_map/legendre_sums/pallas_call | solution.py:278
Async XLA Ops:
  0.0 7.1 %copy-start.1 = (s32[768]{0:T(1024)S(1)}, s32[768]{0:T(1024)}, u32[]{:S(2)}) copy-start(s32[768]{0:T(1024)} %waves.1) | copy-start | bytes 9220
  4.3 22.9 %copy-start = (bf16[120,32,128]{2,1,0:T(8,128)(2,1)S(1)}, bf16[120,32,128]{2,1,0:T(8,128)(2,1)}, u32[]{:S(2)}) copy-start(bf16[120,32,128]{2,1,0:T(8,128)(2,1)} %get-tuple-element.10.held) | copy-start | bytes 2949124
  4.3 22.8 %collective-permute-start = (bf16[60,32,128]{2,1,0:T(8,128)(2,1)}, bf16[60,32,128]{2,1,0:T(8,128)(2,1)S(1)}, u32[]{:S(2)}, u32[]{:S(2)}) collective-permute-start(bf16[60,32,128]{2,1,0:T(8,128)(2,1)} %get-tuple-element.11), channel_id=1, source_target_pairs={{0,2},{4,6},{8,10},{12,14},{16,18},{20,22},{24,26},{28,30},{2,0},{... | collective-permute-start | bytes 1474568 | tf_op jit(solution)/shard_map/ppermute | solution.py:22
  6.4 20.7 %collective-permute-start.1 = (bf16[60,32,128]{2,1,0:T(8,128)(2,1)}, bf16[60,32,128]{2,1,0:T(8,128)(2,1)S(1)}, u32[]{:S(2)}, u32[]{:S(2)}) collective-permute-start(bf16[60,32,128]{2,1,0:T(8,128)(2,1)} %get-tuple-element.12), channel_id=1, source_target_pairs={{2,4},{6,8},{10,12},{14,16},{18,20},{22,24},{26,28},{4,2},{8,6},{1... | collective-permute-start | bytes 1474568 | tf_op jit(solution)/shard_map/ppermute | solution.py:22
  61.2 5.6 %collective-permute-start.2 = (bf16[160,24,128]{2,1,0:T(8,128)(2,1)S(1)}, bf16[160,24,128]{2,1,0:T(8,128)(2,1)S(1)}, u32[]{:S(2)}, u32[]{:S(2)}) collective-permute-start(bf16[160,24,128]{2,1,0:T(8,128)(2,1)S(1)} %bitcast.7), channel_id=1, source_target_pairs={{0,1},{1,0},{2,3},{3,2},{4,5},{5,4},{6,7},{7,6},{8,9},{9,8},{10,11... | collective-permute-start | bytes 2949128 | tf_op jit(solution)/shard_map/ppermute | solution.py:311

commit v4 on v3

v4 whole, which is shorter than its diff:
```python
import functools
import math

import jax
import jax.numpy as jnp
from jax import lax
from jax.experimental import pallas as pl
from jax.experimental.pallas import tpu as pltpu
from jax.sharding import PartitionSpec as P

BF = jnp.bfloat16
F32 = jnp.float32
LANES = 128
MIB = 2**20
A_LIMIT = 56 * MIB
T_LIMIT = 44 * MIB
F_LIMIT = 45 * MIB
W_LIMIT = 45 * MIB
COST = (10**7, 2 * 10**10)
VMEM = pl.BlockSpec(memory_space=pltpu.VMEM)
ANY = pl.BlockSpec(memory_space=pl.ANY)


def exchanged(block, pairs):
    return lax.ppermute(block, "band", pairs + [(j, i) for i, j in pairs])


def interpolate_kernel(
    rim, depart, arrival, tiles, first, second, mid, rows, weights, sums, targets, landed
):
    lats, blocks, width = tiles.shape[0], tiles.shape[1], tiles.shape[2]
    cuts = [lats * i // 3 for i in range(4)]
    arriving = [
        pltpu.make_async_copy(depart, targets, landed.at[0]),
        pltpu.make_async_copy(arrival, rows, landed.at[1]),
    ]
    for i in range(3):
        some = slice(cuts[i], cuts[i + 1])
        arriving.append(
            pltpu.make_async_copy(tiles.at[some], weights.at[some], landed.at[i + 2])
        )
    for copy in arriving:
        copy.start()
    sums[...] = jnp.zeros_like(sums)
    arriving[0].wait()
    arriving[1].wait()
    for i in range(3):
        arriving[i + 2].wait()
        for lat in range(cuts[i], cuts[i + 1]):
            contrib = [
                jnp.dot(
                    rows[lat, :, b * width : (b + 1) * width],
                    weights[lat, b],
                    preferred_element_type=F32,
                )
                for b in range(blocks)
            ]
            for b in range(blocks):
                sums[targets[lat, b]] += contrib[b]
    above = sums.shape[0] - rim
    odd = lax.axis_index("band") % 2
    first[...] = sums[pl.ds(jnp.where(odd == 0, 0, above), rim)].astype(BF)
    second[...] = sums[pl.ds(jnp.where(odd == 0, above, 0), rim)].astype(BF)
    mid[...] = sums[rim:above].astype(BF)


def interpolate(arrival, tiles, depart):
    lats, levels, lons = arrival.shape
    blocks, width = tiles.shape[1], tiles.shape[2]
    rim = lats // 2 * blocks
    segments = lats * blocks + 2 * rim
    return pl.pallas_call(
        functools.partial(interpolate_kernel, rim),
        in_specs=[ANY, ANY, ANY],
        out_specs=[VMEM, VMEM, VMEM],
        out_shape=[
            jax.ShapeDtypeStruct((rim, levels, width), BF),
            jax.ShapeDtypeStruct((rim, levels, width), BF),
            jax.ShapeDtypeStruct((segments - 2 * rim, levels, width), BF),
        ],
        scratch_shapes=[
            pltpu.VMEM(arrival.shape, BF),
            pltpu.VMEM(tiles.shape, BF),
            pltpu.VMEM((segments, levels, width), F32),
            pltpu.SMEM(depart.shape, jnp.int32),
            pltpu.SemaphoreType.DMA((5,)),
        ],
        compiler_params=pltpu.CompilerParams(vmem_limit_bytes=A_LIMIT),
        cost_estimate=pl.CostEstimate(
            flops=2 * lats * levels * lons * width,
            bytes_accessed=2 * (arrival.size + tiles.size),
            transcendentals=0,
        ),
        name="interpolate",
    )(depart, arrival, tiles)


def table_kernel(lons, waves, away, table, copied, near, columns, left):
    fetching = pltpu.make_async_copy(away, near, left.at[2])
    fetching.start()
    blocks = lons // LANES
    halves, _, rows, _ = table.shape
    lane = lax.broadcasted_iota(jnp.int32, (LANES, LANES), 1)
    on_diagonal = lane == lax.broadcasted_iota(jnp.int32, (LANES, LANES), 0)
    for i in range(waves.shape[0]):
        row = jnp.broadcast_to(waves[i : i + 1].astype(F32), (LANES, LANES))
        column = jnp.sum(jnp.where(on_diagonal, row, 0.0), axis=1, keepdims=True)
        columns[i * LANES : (i + 1) * LANES] = jnp.broadcast_to(column, (LANES, LANES))
    step = lax.broadcasted_iota(jnp.int32, (rows, LANES), 1).astype(F32)

    def turn(steps, period):
        left = steps - period * jnp.floor((steps + 0.5) * (1.0 / period))
        angle = left * (2.0 * math.pi / period)
        return jnp.cos(angle), jnp.sin(angle)

    factor = math.sqrt(2.0 / lons)
    leaving = []
    for h in range(halves):
        product = step * columns[pl.ds(h, rows, stride=halves), :]
        fine_cos, fine_sin = turn(product, float(lons))
        coarse_cos, coarse_sin = turn(product, float(blocks))
        coarse_cos = coarse_cos * factor
        coarse_sin = coarse_sin * factor
        for b in range(blocks):
            cos_b, sin_b = coarse_cos[:, b : b + 1], coarse_sin[:, b : b + 1]
            at = slice(b * LANES, (b + 1) * LANES)
            table[h, 0, :, at] = (cos_b * fine_cos - sin_b * fine_sin).astype(BF)
            table[h, 1, :, at] = (sin_b * fine_cos + cos_b * fine_sin).astype(BF)
        leaving.append(pltpu.make_async_copy(table.at[h], copied.at[h], left.at[h]))
        leaving[h].start()
    fetching.wait()
    for copy in leaving:
        copy.wait()


def wave_table(waves, lons, held):
    count = waves.shape[0] // 2
    shape = jax.ShapeDtypeStruct((2, 2, count, lons), BF)
    return pl.pallas_call(
        functools.partial(table_kernel, lons),
        in_specs=[VMEM, ANY],
        out_specs=[VMEM, ANY, VMEM],
        out_shape=[shape, shape, jax.ShapeDtypeStruct(held.shape, held.dtype)],
        scratch_shapes=[pltpu.VMEM((2 * count, LANES), F32), pltpu.SemaphoreType.DMA((3,))],
        compiler_params=pltpu.CompilerParams(vmem_limit_bytes=W_LIMIT),
        cost_estimate=pl.CostEstimate(
            flops=80 * count * lons, bytes_accessed=16 * count * lons, transcendentals=0
        ),
        name="table",
    )(waves.reshape(-1, LANES), held)


def fourier_kernel(phase, held, rims, table, sent, grid, sums):
    rim, levels, width = rims.shape
    bands, lats, half, _ = sent.shape
    odd = lax.axis_index("band") % 2
    start = jnp.where(odd == phase, 0, rim)
    blocks = rim // lats
    per_row = LANES // levels
    parts = table.shape[0]
    groups = pl.cdiv(lats, per_row)

    for lat in range(lats):
        group, place = lat // per_row, lat % per_row
        for b in range(blocks):
            seg = lat * blocks + b
            row = (held[start + seg].astype(F32) + rims[seg].astype(F32)).astype(BF)
            for k in range(parts):
                at = group * LANES + (place + k) % per_row * levels
                grid[k, at : at + levels, b * width : (b + 1) * width] = row

    for k in range(parts):
        sums[k] = lax.dot_general(
            table[k], grid[k], (((1,), (1,)), ((), ())), preferred_element_type=F32
        )
    index = lax.broadcasted_iota(jnp.int32, (half, LANES), 1)
    lane = index // levels
    part = lane // 2 * 2 + index % 2
    level = index % (2 * levels) // 2
    for d in range(bands):
        for group in range(groups):
            pieces = [
                sums[k, d * half : (d + 1) * half, group * LANES : (group + 1) * LANES]
                for k in range(parts)
            ]
            for place in range(min(per_row, lats - group * per_row)):
                row = pieces[(0 - place) % per_row]
                for p in range(1, per_row):
                    row = jnp.where(lane == p, pieces[(p - place) % per_row], row)
                source = (part + place) % per_row * levels + level
                row = jnp.take_along_axis(row, source, axis=1, mode="promise_in_bounds")
                sent[d, group * per_row + place] = row.astype(BF)


def fourier(phase, held, rims, table, bands, flops):
    rim, levels, width = rims.shape
    halves, _, count, lons = table.shape
    lats = rim * width // lons
    half = count // bands
    parts = 2 * halves
    groups = pl.cdiv(lats * levels, LANES)
    return pl.pallas_call(
        functools.partial(fourier_kernel, phase),
        in_specs=[VMEM] * 3,
        out_specs=VMEM,
        out_shape=jax.ShapeDtypeStruct((bands, lats, half, LANES), BF),
        scratch_shapes=[
            pltpu.VMEM((parts, groups * LANES, lons), BF),
            pltpu.VMEM((parts, count, groups * LANES), F32),
        ],
        compiler_params=pltpu.CompilerParams(vmem_limit_bytes=14 * MIB),
        cost_estimate=pl.CostEstimate(flops=flops, bytes_accessed=0, transcendentals=0),
        name="fourier",
    )(held, rims, table.reshape(parts, count, lons))


def lay_out(phases, wide, bands):
    lats, half, lanes = phases[0].shape
    each = lats // bands
    for b in range(bands):
        for side in range(2):
            rows = phases[side ^ (b % 2)][b * each : (b + 1) * each].astype(F32)
            at = (2 * b + side) * each * half
            wide[at : at + each * half] = rows.reshape(each * half, lanes)


def fetch_kernel(source, target, landed):
    copy = pltpu.make_async_copy(source, target, landed)
    copy.start()
    copy.wait()


def fetched(table):
    return pl.pallas_call(
        fetch_kernel,
        in_specs=[ANY],
        out_specs=VMEM,
        out_shape=jax.ShapeDtypeStruct(table.shape, table.dtype),
        scratch_shapes=[pltpu.SemaphoreType.DMA],
        compiler_params=pltpu.CompilerParams(vmem_limit_bytes=T_LIMIT),
        cost_estimate=pl.CostEstimate(flops=0, bytes_accessed=4 * table.size, transcendentals=0),
        name="fetch",
    )(table)


def turn_kernel(bands, early, late, legendre, turned, table, wide, landed):
    half, _, lats = turned.shape
    copy = pltpu.make_async_copy(legendre.at[: table.shape[0]], table, landed)
    copy.start()
    lay_out((early, late), wide, bands)
    for r in range(half):
        turned[r] = wide[pl.ds(r, lats, stride=half), :].T.astype(BF)
    copy.wait()


def turn(early, late, legendre, bands):
    lats, half, lanes = early.shape
    lats = 2 * lats
    return pl.pallas_call(
        functools.partial(turn_kernel, bands),
        in_specs=[VMEM, VMEM, ANY],
        out_specs=[VMEM, VMEM],
        out_shape=[
            jax.ShapeDtypeStruct((half, lanes, lats), BF),
            jax.ShapeDtypeStruct((legendre.shape[0] // 2, *legendre.shape[1:]), BF),
        ],
        scratch_shapes=[pltpu.VMEM((lats * half, lanes), F32), pltpu.SemaphoreType.DMA],
        compiler_params=pltpu.CompilerParams(vmem_limit_bytes=T_LIMIT),
        cost_estimate=pl.CostEstimate(
            flops=0, bytes_accessed=8 * early.size + 2 * legendre.size, transcendentals=0
        ),
        name="turn",
    )(early, late, legendre)


def legendre_kernel(
    bands, waves, own, early, late, near, legendre, out, wide, staged, far, wave, landed, left
):
    half, lanes, lats = own.shape
    levels = lanes // 4
    side = lanes // 2
    degrees = legendre.shape[2]
    split = near.shape[0]
    rest = pltpu.make_async_copy(legendre.at[split:], far, landed.at[1])
    rest.start()
    arriving = pltpu.make_async_copy(waves, wave, landed.at[0])
    arriving.start()
    lay_out((early, late), wide, bands)
    lev = lax.axis_index("lev")
    owned = lax.axis_index("band") * 2 * half
    column = lax.broadcasted_iota(jnp.int32, (lanes, degrees), 1) + lev * degrees
    places = [lev * levels, (1 - lev) * levels]
    arriving.wait()
    leaving = []
    count = half // left.shape[0]
    for c in range(left.shape[0]):
        for r in range(c * count, (c + 1) * count):
            turned = wide[pl.ds(r, lats, stride=half), :].T.astype(BF)
            if r == split // 2:
                rest.wait()
            for slot in range(2):
                at = slice(slot * side, (slot + 1) * side)
                sums = jnp.dot(
                    jnp.concatenate([own[r, at], turned[at]], axis=0),
                    (near[2 * r + slot] if 2 * r + slot < split else far[2 * r + slot - split]),
                    preferred_element_type=F32,
                )
                keep = column >= wave[owned + 2 * r + slot]
                sums = jnp.where(keep, sums, 0.0).astype(BF).reshape(2, levels, 2, degrees)
                for core in range(2):
                    staged[r, slot, pl.ds(places[core], levels)] = sums[core]
        some = slice(c * count, (c + 1) * count)
        leaving.append(pltpu.make_async_copy(staged.at[some], out.at[some], left.at[c]))
        leaving[c].start()
    for copy in leaving:
        copy.wait()


def legendre_sums(own, early, late, near, legendre, waves, bands):
    slots, lats, degrees = legendre.shape
    half, lanes = own.shape[:2]
    levels = lanes // 4
    return pl.pallas_call(
        functools.partial(legendre_kernel, bands),
        in_specs=[ANY, VMEM, VMEM, VMEM, VMEM, ANY],
        out_specs=ANY,
        out_shape=jax.ShapeDtypeStruct((half, 2, 2 * levels, 2, degrees), BF),
        scratch_shapes=[
            pltpu.VMEM((lats * half, lanes), F32),
            pltpu.VMEM((half, 2, 2 * levels, 2, degrees), BF),
            pltpu.VMEM((slots - near.shape[0], lats, degrees), BF),
            pltpu.SMEM(waves.shape, jnp.int32),
            pltpu.SemaphoreType.DMA((2,)),
            pltpu.SemaphoreType.DMA((math.gcd(half, 6),)),
        ],
        compiler_params=pltpu.CompilerParams(vmem_limit_bytes=F_LIMIT),
        cost_estimate=pl.CostEstimate(
            flops=2 * slots * lats * lanes * degrees,
            bytes_accessed=2 * slots * lanes * degrees,
            transcendentals=0,
        ),
        name="legendre_sums",
    )(waves, own, early, late, near, legendre)


def local(arrival_adjoint, interp_tiles, departure_block, slot_wavenumber, legendre):
    lons = arrival_adjoint.shape[2]
    slots = legendre.shape[0]
    bands = lax.axis_size("band")
    first, second, held = interpolate(arrival_adjoint, interp_tiles, departure_block)
    first = exchanged(first, [(i, i + 1) for i in range(1, bands - 1, 2)])
    table, copied, held = wave_table(slot_wavenumber, lons, held)
    first, second, copied = lax.optimization_barrier((first, second, copied))
    second = exchanged(second, [(i, i + 1) for i in range(0, bands - 1, 2)])

    def owned(sent):
        own = lax.all_to_all(sent, "band", split_axis=0, concat_axis=0)
        return own.reshape(-1, *own.shape[2:])

    def other(own):
        return lax.ppermute(own, "lev", [(0, 1), (1, 0)])

    sent, copied = lax.optimization_barrier(
        (fourier(0, held, first, table, bands, COST[0]), copied)
    )
    own_early = owned(sent)
    early = other(own_early)
    second, table = lax.optimization_barrier((second, fetched(copied)))
    own_late = owned(fourier(1, held, second, table, bands, COST[1]))
    late = other(own_late)
    own, near = turn(own_early, own_late, legendre, bands)
    done = legendre_sums(own, early, late, near, legendre, slot_wavenumber, bands)
    return done.reshape(slots, done.shape[2], 2, done.shape[4])


def solution(mesh):
    placed = (
        P("band", "lev", None),
        P("band", None, None, None),
        P("band", None),
        P(),
        P("band", None, "lev"),
    )
    return jax.shard_map(
        local, mesh=mesh, in_specs=placed, out_specs=P("band", None, None, "lev"), check_vma=False
    )
```

time: 70.5 us -> 68.5 us (0.972)
  blocking collectives: 30.5 us -> 0 us
  starting transfers between devices: 5.7 us -> 27.1 us
  Pallas kernels: 19.8 us -> 23.5 us
  waiting for transfers between devices: 11.6 us -> 13.6 us
  local copies, waits for them, and re-layouts: 2.72 us -> 3.53 us
    all_to_all x1 -> x0, blocking collectives: 30.5 us -> none  [local(): own = lax.all_to_all(sent, 'band', split_axis=0, concat_axis=0)]
    all_to_all x0 -> x2, waiting for transfers between devices: none -> 13.6 us  [owned(): own = lax.all_to_all(sent, 'band', split_axis=0, concat_axis=0)]
    all_to_all x0 -> x2, starting transfers between devices: none -> 12 us  [owned(): own = lax.all_to_all(sent, 'band', split_axis=0, concat_axis=0)]
    ppermute x2, waiting for transfers between devices: 11.6 us -> 0.01 us  [exchanged(): return lax.ppermute(block, 'band', pairs + [(j, i) for i, j in pairs])]
    ppermute x2, starting transfers between devices: 2.79 us -> 7.85 us  [exchanged(): return lax.ppermute(block, 'band', pairs + [(j, i) for i, j in pairs])]
    ppermute x1 -> x2, starting transfers between devices: 2.91 us -> 7.32 us  [other(): return lax.ppermute(own, 'lev', [(0, 1), (1, 0)])]
    pallas_call x4 -> x6, Pallas kernels: 15.4 us -> 19.2 us  [the longest x1 8.05 us: wave_table(): pl.pallas_call(functools.partial(table_kernel, lons), in_specs=[VMEM, ANY...]
    unnamed x4 -> x6, local copies, waits for them, and re-layouts: 0.01 us -> 3.53 us
  transfers between devices with their start and end apart: 3 -> 6, of which waited for: 1 -> 2; matrix products, arithmetic and copies ran while one was open for 4% -> 0% of each run, Pallas kernels for 12% -> 23%
where the time goes in v4:
time: 68.5 us; the launch traced here: 68.1 us
  starting transfers between devices  27.1 us (40%)
  Pallas kernels  23.5 us (34%)
  waiting for transfers between devices  13.6 us (20%)
  local copies, waits for them, and re-layouts  3.53 us (5%)
    all_to_all x2, waiting for transfers between devices, owned(): own = lax.all_to_all(sent, 'band', split_axis=0, concat_axis=0)  13.6 us
    all_to_all x2, starting transfers between devices, owned(): own = lax.all_to_all(sent, 'band', split_axis=0, concat_axis=0)  12 us
    pallas_call x1, Pallas kernels, wave_table(): pl.pallas_call(functools.partial(table_kernel, lons), in_specs=[VMEM, ANY...  8.05 us
    ppermute x2, starting transfers between devices, exchanged(): return lax.ppermute(block, 'band', pairs + [(j, i) for i, j in pairs])  7.85 us
    ppermute x2, starting transfers between devices, other(): return lax.ppermute(own, 'lev', [(0, 1), (1, 0)])  7.32 us
    pallas_call x2, Pallas kernels, fourier(): pl.pallas_call(functools.partial(fourier_kernel, phase), in_specs=[VMEM]...  5.13 us
    pallas_call x1, Pallas kernels, interpolate(): pl.pallas_call(functools.partial(interpolate_kernel, rim), in_specs=[ANY,...  4.32 us
    pallas_call x1, Pallas kernels, legendre_sums(): pl.pallas_call(functools.partial(legendre_kernel, bands), in_specs=[ANY,...  3.84 us
  transfers between devices with their start and end apart: 6, of which 2 were waited for; matrix products, arithmetic and copies ran while one was open for 0% of the time, Pallas kernels for 23%

profile of v4, /device:TPU:1, one launch (start us, length us, event | category | flops | bytes accessed | tf_op | source)
XLA Modules:
  0.0 68.1 jit_solution(6757950085112597932)
XLA Ops:
  0.0 0.0 copy-start.2
  0.0 4.3 %interpolate.1 = (bf16[60,32,128]{2,1,0:T(8,128)(2,1)}, bf16[60,32,128]{2,1,0:T(8,128)(2,1)}, bf16[120,32,128]{2,1,0:T(8,128)(2,1)}) custom-call(s32[10,12]{1,0:T(8,128)} %depart.1, bf16[10,32,1536]{2,1,0:T(8,128)(2,1)} %arrival.1, bf16[10,12,128,128]{3,2,1,0:T(8,128)(2,1)} %tiles.1), custom_call_target="tpu_custom_call" | custom-call | flops 125829120 | bytes 4915200 | tf_op jit(solution)/shard_map/interpolate/pallas_call | solution.py:72
  4.3 0.7 %collective-permute-start = (bf16[60,32,128]{2,1,0:T(8,128)(2,1)}, bf16[60,32,128]{2,1,0:T(8,128)(2,1)S(1)}, u32[]{:S(2)}, u32[]{:S(2)}) collective-permute-start(bf16[60,32,128]{2,1,0:T(8,128)(2,1)} %get-tuple-element.22), channel_id=1, source_target_pairs={{2,4},{6,8},{10,12},{14,16},{18,20},{22,24},{26,28},{4,2},{8,6},{1... | collective-permute-start | bytes 1474568 | tf_op jit(solution)/shard_map/ppermute | solution.py:25
  5.0 0.0 copy-done.2
  5.0 0.0 copy-start.1
  5.1 1.2 %copy-done.1 = bf16[120,32,128]{2,1,0:T(8,128)(2,1)S(1)} copy-done((bf16[120,32,128]{2,1,0:T(8,128)(2,1)S(1)}, bf16[120,32,128]{2,1,0:T(8,128)(2,1)}, u32[]{:S(2)}) %copy-start.1) | copy-done | bytes 983064
  6.2 8.0 %table.1 = (bf16[2,2,384,1536]{3,2,1,0:T(8,128)(2,1)S(1)}, bf16[2,2,384,1536]{3,2,1,0:T(8,128)(2,1)}, bf16[120,32,128]{2,1,0:T(8,128)(2,1)S(1)}) custom-call(s32[6,128]{1,0:T(8,128)S(1)} %bitcast.12, bf16[120,32,128]{2,1,0:T(8,128)(2,1)S(1)} %copy-done.1), custom_call_target="tpu_custom_call" | custom-call | flops 47185920 | bytes 9437184 | tf_op jit(solution)/shard_map/table/pallas_call | solution.py:139
  14.3 0.0 collective-permute-done.rims
  14.3 7.2 %collective-permute-start.1 = (bf16[60,32,128]{2,1,0:T(8,128)(2,1)}, bf16[60,32,128]{2,1,0:T(8,128)(2,1)S(1)}, u32[]{:S(2)}, u32[]{:S(2)}) collective-permute-start(bf16[60,32,128]{2,1,0:T(8,128)(2,1)} %get-tuple-element.29), channel_id=1, source_target_pairs={{0,2},{4,6},{8,10},{12,14},{16,18},{20,22},{24,26},{28,30},{2,0},{... | collective-permute-start | bytes 1474568 | tf_op jit(solution)/shard_map/ppermute | solution.py:25
  21.5 2.6 %fourier.2 = bf16[16,5,24,128]{3,2,1,0:T(8,128)(2,1)} custom-call(bf16[120,32,128]{2,1,0:T(8,128)(2,1)S(1)} %get-tuple-element.21.held, bf16[60,32,128]{2,1,0:T(8,128)(2,1)S(1)} %collective-permute-done.rims, bf16[4,384,1536]{2,1,0:T(8,128)(2,1)S(1)} %bitcast.6), custom_call_target="tpu_custom_call" | custom-call | flops 10000000 | tf_op jit(solution)/shard_map/fourier/pallas_call | solution.py:202
  24.0 5.6 %all-to-all-start = ((bf16[16,5,24,128]{3,2,1,0:T(8,128)(2,1)}), bf16[16,5,24,128]{3,2,1,0:T(8,128)(2,1)S(1)}, u32[]{:S(2)}, u32[]{:S(2)}) async-start(bf16[16,5,24,128]{3,2,1,0:T(8,128)(2,1)} %fourier.2), calls=%async_computation | async-start | bytes 983040 | tf_op jit(solution)/shard_map/all_to_all | solution.py:357
  29.7 0.0 copy-start
  29.7 2.3 %copy-done = bf16[2,2,384,1536]{3,2,1,0:T(8,128)(2,1)S(1)} copy-done((bf16[2,2,384,1536]{3,2,1,0:T(8,128)(2,1)S(1)}, bf16[2,2,384,1536]{3,2,1,0:T(8,128)(2,1)}, u32[]{:S(2)}) %copy-start) | copy-done | bytes 4718616
  32.0 0.3 fetch.1
  32.3 0.0 collective-permute-done.1.rims
  32.4 2.6 %fourier.3 = bf16[16,5,24,128]{3,2,1,0:T(8,128)(2,1)} custom-call(bf16[120,32,128]{2,1,0:T(8,128)(2,1)S(1)} %get-tuple-element.21.held, bf16[60,32,128]{2,1,0:T(8,128)(2,1)S(1)} %collective-permute-done.1.rims, bf16[4,384,1536]{2,1,0:T(8,128)(2,1)S(1)} %bitcast.7), custom_call_target="tpu_custom_call" | custom-call | flops 20000000000 | tf_op jit(solution)/shard_map/fourier/pallas_call | solution.py:202
  34.9 5.4 %all-to-all-done = bf16[16,5,24,128]{3,2,1,0:T(8,128)(2,1)S(1)} async-done(((bf16[16,5,24,128]{3,2,1,0:T(8,128)(2,1)}), bf16[16,5,24,128]{3,2,1,0:T(8,128)(2,1)S(1)}, u32[]{:S(2)}, u32[]{:S(2)}) %all-to-all-start) | async-done | bytes 491552 | tf_op jit(solution)/shard_map/all_to_all | solution.py:357
  40.3 6.3 %all-to-all-start.1 = ((bf16[16,5,24,128]{3,2,1,0:T(8,128)(2,1)}), bf16[16,5,24,128]{3,2,1,0:T(8,128)(2,1)S(1)}, u32[]{:S(2)}, u32[]{:S(2)}) async-start(bf16[16,5,24,128]{3,2,1,0:T(8,128)(2,1)} %fourier.3), calls=%async_computation.1 | async-start | bytes 983040 | tf_op jit(solution)/shard_map/all_to_all | solution.py:357
  46.7 2.4 %collective-permute-start.2 = (bf16[80,24,128]{2,1,0:T(8,128)(2,1)S(1)}, bf16[80,24,128]{2,1,0:T(8,128)(2,1)S(1)}, u32[]{:S(2)}, u32[]{:S(2)}) collective-permute-start(bf16[80,24,128]{2,1,0:T(8,128)(2,1)S(1)} %bitcast.8), channel_id=1, source_target_pairs={{0,1},{1,0},{2,3},{3,2},{4,5},{5,4},{6,7},{7,6},{8,9},{9,8},{10,11... | collective-permute-start | bytes 1474568 | tf_op jit(solution)/shard_map/ppermute | solution.py:361
  49.0 8.2 %all-to-all-done.1 = bf16[16,5,24,128]{3,2,1,0:T(8,128)(2,1)S(1)} async-done(((bf16[16,5,24,128]{3,2,1,0:T(8,128)(2,1)}), bf16[16,5,24,128]{3,2,1,0:T(8,128)(2,1)S(1)}, u32[]{:S(2)}, u32[]{:S(2)}) %all-to-all-start.1) | async-done | bytes 491552 | tf_op jit(solution)/shard_map/all_to_all | solution.py:357
  57.2 5.0 %collective-permute-start.3 = (bf16[80,24,128]{2,1,0:T(8,128)(2,1)S(1)}, bf16[80,24,128]{2,1,0:T(8,128)(2,1)S(1)}, u32[]{:S(2)}, u32[]{:S(2)}) collective-permute-start(bf16[80,24,128]{2,1,0:T(8,128)(2,1)S(1)} %bitcast.10), channel_id=1, source_target_pairs={{0,1},{1,0},{2,3},{3,2},{4,5},{5,4},{6,7},{7,6},{8,9},{9,8},{10,11... | collective-permute-start | bytes 1474568 | tf_op jit(solution)/shard_map/ppermute | solution.py:361
  62.2 1.8 %turn.1 = (bf16[24,128,160]{2,1,0:T(8,128)(2,1)S(1)}, bf16[24,160,384]{2,1,0:T(8,128)(2,1)S(1)}) custom-call(bf16[80,24,128]{2,1,0:T(8,128)(2,1)S(1)} %bitcast.9, bf16[80,24,128]{2,1,0:T(8,128)(2,1)S(1)} %bitcast.11, bf16[48,160,384]{2,1,0:T(8,128)(2,1)} %legendre.3), custom_call_target="tpu_custom_call" | custom-call | bytes 7864320 | tf_op jit(solution)/shard_map/turn/pallas_call | solution.py:259
  64.0 0.0 collective-permute-done.2.early
  64.0 0.0 collective-permute-done.3.late
  64.1 3.8 %legendre_sums.1 = bf16[24,2,64,2,384]{4,3,2,1,0:T(2,128)(2,1)} custom-call(s32[768]{0:T(1024)S(1)} %copy-done.2, bf16[24,128,160]{2,1,0:T(8,128)(2,1)S(1)} %get-tuple-element.33.own, bf16[80,24,128]{2,1,0:T(8,128)(2,1)S(1)} %collective-permute-done.2.early, bf16[80,24,128]{2,1,0:T(8,128)(2,1)S(1)} %collective-permute-done.3.late, ...), custom_call_target="tpu_custom_call" | custom-call | flops 754974720 | bytes 4718592 | tf_op jit(solution)/shard_map/legendre_sums/pallas_call | solution.py:323
Async XLA Ops:
  0.0 5.0 %copy-start.2 = (s32[768]{0:T(1024)S(1)}, s32[768]{0:T(1024)}, u32[]{:S(2)}) copy-start(s32[768]{0:T(1024)} %waves.1) | copy-start | bytes 9220
  4.3 10.0 %collective-permute-start = (bf16[60,32,128]{2,1,0:T(8,128)(2,1)}, bf16[60,32,128]{2,1,0:T(8,128)(2,1)S(1)}, u32[]{:S(2)}, u32[]{:S(2)}) collective-permute-start(bf16[60,32,128]{2,1,0:T(8,128)(2,1)} %get-tuple-element.22), channel_id=1, source_target_pairs={{2,4},{6,8},{10,12},{14,16},{18,20},{22,24},{26,28},{4,2},{8,6},{1... | collective-permute-start | bytes 1474568 | tf_op jit(solution)/shard_map/ppermute | solution.py:25
  5.0 1.2 %copy-start.1 = (bf16[120,32,128]{2,1,0:T(8,128)(2,1)S(1)}, bf16[120,32,128]{2,1,0:T(8,128)(2,1)}, u32[]{:S(2)}) copy-start(bf16[120,32,128]{2,1,0:T(8,128)(2,1)} %get-tuple-element.20.away) | copy-start | bytes 2949124
  14.3 18.0 %collective-permute-start.1 = (bf16[60,32,128]{2,1,0:T(8,128)(2,1)}, bf16[60,32,128]{2,1,0:T(8,128)(2,1)S(1)}, u32[]{:S(2)}, u32[]{:S(2)}) collective-permute-start(bf16[60,32,128]{2,1,0:T(8,128)(2,1)} %get-tuple-element.29), channel_id=1, source_target_pairs={{0,2},{4,6},{8,10},{12,14},{16,18},{20,22},{24,26},{28,30},{2,0},{... | collective-permute-start | bytes 1474568 | tf_op jit(solution)/shard_map/ppermute | solution.py:25
  24.0 16.3 %all-to-all-start = ((bf16[16,5,24,128]{3,2,1,0:T(8,128)(2,1)}), bf16[16,5,24,128]{3,2,1,0:T(8,128)(2,1)S(1)}, u32[]{:S(2)}, u32[]{:S(2)}) async-start(bf16[16,5,24,128]{3,2,1,0:T(8,128)(2,1)} %fourier.2), calls=%async_computation | async-start | bytes 983040 | tf_op jit(solution)/shard_map/all_to_all | solution.py:357
  29.7 2.3 %copy-start = (bf16[2,2,384,1536]{3,2,1,0:T(8,128)(2,1)S(1)}, bf16[2,2,384,1536]{3,2,1,0:T(8,128)(2,1)}, u32[]{:S(2)}) copy-start(bf16[2,2,384,1536]{3,2,1,0:T(8,128)(2,1)} %get-tuple-element.30.source) | copy-start | bytes 14155780
  40.3 16.9 %all-to-all-start.1 = ((bf16[16,5,24,128]{3,2,1,0:T(8,128)(2,1)}), bf16[16,5,24,128]{3,2,1,0:T(8,128)(2,1)S(1)}, u32[]{:S(2)}, u32[]{:S(2)}) async-start(bf16[16,5,24,128]{3,2,1,0:T(8,128)(2,1)} %fourier.3), calls=%async_computation.1 | async-start | bytes 983040 | tf_op jit(solution)/shard_map/all_to_all | solution.py:357
  46.7 17.3 %collective-permute-start.2 = (bf16[80,24,128]{2,1,0:T(8,128)(2,1)S(1)}, bf16[80,24,128]{2,1,0:T(8,128)(2,1)S(1)}, u32[]{:S(2)}, u32[]{:S(2)}) collective-permute-start(bf16[80,24,128]{2,1,0:T(8,128)(2,1)S(1)} %bitcast.8), channel_id=1, source_target_pairs={{0,1},{1,0},{2,3},{3,2},{4,5},{5,4},{6,7},{7,6},{8,9},{9,8},{10,11... | collective-permute-start | bytes 1474568 | tf_op jit(solution)/shard_map/ppermute | solution.py:361
  57.2 6.8 %collective-permute-start.3 = (bf16[80,24,128]{2,1,0:T(8,128)(2,1)S(1)}, bf16[80,24,128]{2,1,0:T(8,128)(2,1)S(1)}, u32[]{:S(2)}, u32[]{:S(2)}) collective-permute-start(bf16[80,24,128]{2,1,0:T(8,128)(2,1)S(1)} %bitcast.10), channel_id=1, source_target_pairs={{0,1},{1,0},{2,3},{3,2},{4,5},{5,4},{6,7},{7,6},{8,9},{9,8},{10,11... | collective-permute-start | bytes 1474568 | tf_op jit(solution)/shard_map/ppermute | solution.py:361
